TPU v7x, 32 devices: a whole 2x2x4 slice. The times are simulated.
32 devices in a mesh: groups: 2 (over x), feat: 16 (over z, y, core).
Axes of the slice: x: 2, y: 2, z: 4, core: 2. Of those that a mesh axis runs over, the one named last changes fastest.
Arguments:
- design: float32 [1024, 32768], P('groups', 'feat'), parts along dimension 0, may hold values from -6 to 6
- targets: float32 [1024, 128], P('groups'), parts along dimension 0, may hold values from -6 to 6
- coef_now: float32 [65536, 128], P(('groups', 'feat')), parts along dimension 0, may hold values from -1 to 1
- coef_prev: float32 [65536, 128], P(('groups', 'feat')), parts along dimension 0, may hold values from -1 to 1
- penalty: float32 [256], P('groups'), parts along dimension 0, may hold values from 0.1 to 1
- drop_mask: int32 [512], P(('groups', 'feat')), parts along dimension 0, may hold values from 0 to 1, as said below
- dest_shard: int32 [512], P(('groups', 'feat')), parts along dimension 0, may hold values from 0 to 15, as said below
Outputs:
- coef_out: float32 [98304, 128], P(('groups', 'feat')), parts along dimension 0
- design_out: float32 [1024, 49152], P('groups', 'feat'), parts along dimension 0
- duality_gap: float32 [256], P('groups'), parts along dimension 0
- dual_value: float32 [256], P('groups'), parts along dimension 0
- coef_l1: float32 [256], P('groups'), parts along dimension 0
There are 2 independent parts, one for each index of `groups`. A program takes and returns all parts, laid end to end along the dimension named above; each array names one. Nothing has to cross between parts.
Inputs may be any that keep to these rules, and one draw needn't show every extreme that they name: `drop_mask`: screening marks blocks to drop with 1; shards drop very different shares of their blocks. `dest_shard`: a block's destination is its own shard, except that any of the first 4 blocks of a shard may go to the shard before it (cyclically) and any of the last 4 blocks to the shard after it; no shard receives more than 24 surviving blocks, and some shard receives exactly 24 in every draw.
All inputs are finite; a program needn't handle non-finite values.
Results may differ from a plain program's by a relative error of at most 0.0003.
Values sent between devices are 32-bit elements; how exact they have to be, the bound alone decides.
No kernel may reach another device: no remote copies, remote signals or barrier semaphores. Data moves between devices by JAX's collectives and lax.ppermute only.
A program may use at most 64 MiB of HBM per device.

v0:
```python
import math

import jax
import jax.numpy as jnp
from jax import lax
from jax.sharding import PartitionSpec as P

START = 40


precise = lax.Precision.HIGHEST


def shifted(value, axis, steps):
    count = lax.axis_size(axis)
    pairs = [(source, (source + steps) % count) for source in range(count)]
    return lax.ppermute(value, axis, pairs)


def shrink(values, level):
    return jnp.sign(values) * jnp.maximum(jnp.abs(values) - level, 0.0)


def local(design, targets, coef_now, coef_prev, penalty, drop_mask, dest_shard):
    sample_count, local_feats = design.shape
    shards = lax.axis_size("feat")
    my_index = lax.axis_index("feat")
    lipschitz = (math.sqrt(sample_count) + math.sqrt(local_feats * shards)) ** 2
    level = penalty * (sample_count / lipschitz)
    first_push = (START - 1) / (START + 2)
    second_push = START / (START + 3)
    block_count = local_feats // 128
    edge_count = block_count // 4
    survive = drop_mask == 0
    to_left = survive[:edge_count] & (dest_shard[:edge_count] == (my_index + shards - 1) % shards)
    to_right = survive[block_count - edge_count :] & (
        dest_shard[block_count - edge_count :] == (my_index + 1) % shards
    )
    staying = survive & (dest_shard == my_index)
    left_flags = to_left.astype(jnp.int32)
    right_flags = to_right.astype(jnp.int32)
    design_blocks = design.reshape(sample_count, block_count, 128)
    left_design = design_blocks[:, :edge_count]
    right_design = design_blocks[:, block_count - edge_count :]

    def misfit_of(point):
        row_count = sample_count // shards
        fitted_rows = lax.psum_scatter(
            jnp.dot(design, point, precision=precise, preferred_element_type=jnp.float32),
            "feat",
            scatter_dimension=0,
            tiled=True,
        )
        own_targets = lax.dynamic_slice_in_dim(targets, my_index * row_count, row_count, 0)
        misfit = lax.all_gather(fitted_rows - own_targets, "feat", axis=0, tiled=True)
        return misfit

    def correlate(misfit):
        return lax.dot_general(
            design,
            misfit,
            (((0,), (0,)), ((), ())),
            precision=precise,
            preferred_element_type=jnp.float32,
        )

    def descend(point):
        misfit = misfit_of(point)
        return shrink(point - correlate(misfit) / lipschitz, level)

    coef_one = descend(coef_now + first_push * (coef_now - coef_prev))
    coef_two = descend(coef_one + second_push * (coef_one - coef_now))
    residual = -misfit_of(coef_two)
    correlation = correlate(residual)
    local_peak = jnp.max(jnp.abs(correlation), axis=0)
    local_mass = jnp.sum(jnp.abs(coef_two), axis=0)
    peak = lax.pmax(local_peak, "feat")
    mass = lax.psum(local_mass, "feat")
    dual_scale = jnp.maximum(penalty, peak / sample_count)
    dual_point = targets - penalty * residual / dual_scale
    dual_value = (jnp.sum(targets * targets, axis=0) - jnp.sum(dual_point * dual_point, axis=0)) / (
        2.0 * sample_count
    )
    primal = jnp.sum(residual * residual, axis=0) / (2.0 * sample_count) + penalty * mass
    duality_gap = primal - dual_value
    coef_blocks = coef_two.reshape(block_count, 128, coef_two.shape[1])
    left_coef = coef_blocks[:edge_count]
    right_coef = coef_blocks[block_count - edge_count :]
    before_design, before_coef, before_flags = shifted(
        (right_design, right_coef, right_flags), "feat", 1
    )
    after_design, after_coef, after_flags = shifted(
        (left_design, left_coef, left_flags), "feat", -1
    )
    arrived = jnp.concatenate([before_flags, staying.astype(jnp.int32), after_flags])
    slot_total = arrived.shape[0]
    slot_of = jnp.cumsum(arrived, dtype=jnp.int32) - 1
    placement = (
        (slot_of[:, None] == jnp.arange(slot_total, dtype=jnp.int32)[None, :])
        & (arrived[:, None] > 0)
    ).astype(jnp.float32)
    design_cands = jnp.concatenate([before_design, design_blocks, after_design], axis=1)
    design_out = jnp.einsum("ncf,cj->njf", design_cands, placement, precision=precise).reshape(
        sample_count, slot_total * 128
    )
    coef_cands = jnp.concatenate([before_coef, coef_blocks, after_coef], axis=0)
    coef_out = jnp.einsum("cfk,cj->jfk", coef_cands, placement, precision=precise).reshape(
        slot_total * 128, coef_two.shape[1]
    )
    return (coef_out, design_out, duality_gap, dual_value, mass)


def solution(mesh):
    placed = (
        P("groups", "feat"),
        P("groups", None),
        P(("groups", "feat"), None),
        P(("groups", "feat"), None),
        P("groups"),
        P(("groups", "feat")),
        P(("groups", "feat")),
    )
    return jax.shard_map(
        local,
        mesh=mesh,
        in_specs=placed,
        out_specs=(
            P(("groups", "feat"), None),
            P("groups", "feat"),
            P("groups"),
            P("groups"),
            P("groups"),
        ),
        check_vma=False,
    )
```

profile of v0, /device:TPU:0, one launch (start us, length us, event | category | flops | bytes accessed | tf_op | source)
XLA Modules:
  0.0 308.4 jit_solution(12566425344645803964)
XLA Ops:
  7.2 1.6 copy.35
  8.8 1.6 copy.36
  10.4 6.4 %convolution_bitcast_fusion.2 = f32[512,128]{0,1:T(8,128)S(1)} fusion(f32[512,2048]{1,0:T(8,128)} %param.7, f32[2048,128]{0,1:T(8,128)S(1)} %copy.36, f32[2048,128]{0,1:T(8,128)S(1)} %copy.35), kind=kOutput, calls=%fused_computation.23 | convolution fusion | flops 1611399168 | bytes 6553600 | tf_op jit(solution)/shard_map/dot_general | solution.py:49
  18.4 5.0 %collective-permute-start.1 = (s32[4]{0:T(128)S(1)}, s32[4]{0:T(128)S(1)}, u32[]{:S(2)}, u32[]{:S(2)}) collective-permute-start(s32[4]{0:T(128)S(1)} %get-tuple-element.17), channel_id=1, source_target_pairs={{0,15},{1,0},{2,1},{3,2},{4,3},{5,4},{6,5},{7,6},{8,7},{9,8},{10,9... | collective-permute-start | bytes 56 | tf_op jit(solution)/shard_map/ppermute | solution.py:17
  23.5 5.1 %copy.54 = f32[64,8,16,128]{3,2,1,0:T(8,128)} copy(f32[64,8,16,128]{3,1,2,0:T(8,128)} %bitcast.52) | data formatting | bytes 8388608
  28.7 47.7 %reduce-scatter.10.cloned.1.call-done = f32[32,128]{1,0:T(8,128)} async-done(((f32[512,128]{1,0:T(8,128)}), f32[32,128]{1,0:T(8,128)}) %reduce-scatter.10.cloned.1.call-update) | async-done | bytes 16400
  77.2 20.3 %all_gather.9 = f32[512,128]{1,0:T(8,128)S(1)} all-gather(f32[32,128]{1,0:T(8,128)S(1)} %copy.38), channel_id=1, replica_groups=mesh['groups'=2,'feat'=16] {'feat'}, dimensions={0}, use_global_device_ids=true | all-gather | bytes 278528 | tf_op jit(solution)/shard_map/all_gather | solution.py:55
  97.5 5.1 %multiply_add_fusion = f32[2048,128]{0,1:T(8,128)S(1)} fusion(f32[2048,128]{0,1:T(8,128)S(1)} %copy.36, f32[512,128]{1,0:T(8,128)S(1)} %all_gather.9, f32[512,2048]{1,0:T(8,128)} %param.7, f32[2048,128]{0,1:T(8,128)S(1)} %copy.35, f32[128]{0:T(128)S(1)} %broadcast_multiply_fusion), kind=kOutput, calls=%fused_computation.26 | convolution fusion | flops 1614020608 | bytes 7602688 | tf_op jit(solution)/shard_map/dot_general | solution.py:59
  102.6 4.5 %convolution_bitcast_fusion.1 = f32[512,128]{0,1:T(8,128)S(1)} fusion(f32[2048,128]{0,1:T(8,128)S(1)} %multiply_add_fusion, f32[512,2048]{1,0:T(8,128)S(1)} %copy-done), kind=kOutput, calls=%fused_computation.22 | convolution fusion | flops 1610612736 | bytes 5505024 | tf_op jit(solution)/shard_map/dot_general | solution.py:49
  108.2 3.9 %fusion.30 = (f32[512,4,128]{2,1,0:T(4,128)}, f32[512,4,128]{2,1,0:T(4,128)}) fusion(f32[512,16,128]{2,1,0:T(8,128)} %bitcast.53), kind=kLoop, calls=%fused_computation.55 | loop fusion | bytes 4194304 | tf_op jit(solution)/shard_map/slice | solution.py:44
  112.5 4.1 %collective-permute-start.5 = (f32[512,4,128]{2,1,0:T(4,128)}, f32[512,4,128]{2,1,0:T(4,128)}, u32[]{:S(2)}, u32[]{:S(2)}) collective-permute-start(f32[512,4,128]{2,1,0:T(4,128)} %get-tuple-element.13), channel_id=1, source_target_pairs={{0,15},{1,0},{2,1},{3,2},{4,3},{5,4},{6,5},{7,6},{8,7},{9,8},{10,9... | collective-permute-start | bytes 3145736 | tf_op jit(solution)/shard_map/ppermute | solution.py:17
  116.9 44.2 %reduce-scatter.12.cloned.1.call-done = f32[32,128]{1,0:T(8,128)} async-done(((f32[512,128]{1,0:T(8,128)}), f32[32,128]{1,0:T(8,128)}) %reduce-scatter.12.cloned.1.call-update) | async-done | bytes 16400
  162.0 20.3 %all_gather.10 = f32[512,128]{1,0:T(8,128)S(1)} all-gather(f32[32,128]{1,0:T(8,128)S(1)} %copy.40), channel_id=1, replica_groups=mesh['groups'=2,'feat'=16] {'feat'}, dimensions={0}, use_global_device_ids=true | all-gather | bytes 278528 | tf_op jit(solution)/shard_map/all_gather | solution.py:55
  182.3 5.0 %abs_reduce_fusion = (f32[128]{0:T(128)S(1)}, f32[2048,128]{0,1:T(8,128)S(1)}) fusion(f32[128]{0:T(128)S(1)} %broadcast_multiply_fusion, f32[2048,128]{0,1:T(8,128)S(1)} %multiply_add_fusion, f32[512,128]{1,0:T(8,128)S(1)} %all_gather.10, f32[512,2048]{1,0:T(8,128)} %param.7), kind=kOutput, calls=%fused_computation.24 | convolution fusion | flops 1612971904 | bytes 6554624 | tf_op jit(solution)/shard_map/dot_general | solution.py:59
  187.3 4.5 %convolution_bitcast_fusion = f32[512,128]{0,1:T(8,128)S(1)} fusion(f32[2048,128]{0,1:T(8,128)S(1)} %get-tuple-element.21, f32[512,2048]{1,0:T(8,128)S(1)} %copy-done.1), kind=kOutput, calls=%fused_computation.21 | convolution fusion | flops 1610612736 | bytes 5505024 | tf_op jit(solution)/shard_map/dot_general | solution.py:49
  193.6 4.2 %collective-permute-start.3 = (f32[4,128,128]{2,0,1:T(4,128)S(1)}, f32[4,128,128]{2,0,1:T(4,128)S(1)}, u32[]{:S(2)}, u32[]{:S(2)}) collective-permute-start(f32[4,128,128]{2,0,1:T(4,128)S(1)} %copy.42), channel_id=1, source_target_pairs={{0,15},{1,0},{2,1},{3,2},{4,3},{5,4},{6,5},{7,6},{8,7},{9,8},{10,9... | collective-permute-start | bytes 786440 | tf_op jit(solution)/shard_map/ppermute | solution.py:17
  198.7 30.2 %psum.7 = f32[128]{0:T(128)S(1)} all-reduce(f32[128]{0:T(128)S(1)} %get-tuple-element.20), channel_id=1, replica_groups=mesh['groups'=2,'feat'=16] {'feat'}, use_global_device_ids=true, to_apply=%region_6.7 | all-reduce | flops 128 | bytes 1024 | tf_op jit(solution)/shard_map/psum | solution.py:78
  228.9 6.1 %fusion = f32[24,512,128]{2,0,1:T(8,128)S(1)} fusion(f32[512,4,128]{2,1,0:T(4,128)} %collective-permute-done.5, f32[512,16,128]{2,1,0:T(8,128)} %bitcast.54, f32[512,4,128]{2,1,0:T(4,128)} %collective-permute-done.4, s32[24]{0:T(128)S(1)} %add_reduce_fusion, pred[24]{0:T(512)(128)(4,1)S(1)} %get-tuple-element.10), kind=kOutput, calls=%fused_computation.1 | convolution fusion | flops 456131712 | bytes 12583032 | tf_op jit(solution)/shard_map/ncf,cj->njf/dot_general | solution.py:103
  235.0 4.1 %copy.57 = f32[64,8,24,128]{3,1,2,0:T(8,128)} copy(f32[64,8,24,128]{3,2,1,0:T(8,128)S(1)} %bitcast.55) | data formatting | bytes 12582912
  240.1 1.4 copy.44
  241.5 4.3 %reduce-scatter.14.cloned.1.call-done = f32[32,128]{1,0:T(8,128)} async-done(((f32[512,128]{1,0:T(8,128)}), f32[32,128]{1,0:T(8,128)}) %reduce-scatter.14.cloned.1.call-update) | async-done | bytes 16400
  246.6 20.2 %all_gather.11 = f32[512,128]{1,0:T(8,128)S(1)} all-gather(f32[32,128]{1,0:T(8,128)S(1)} %copy.45), channel_id=1, replica_groups=mesh['groups'=2,'feat'=16] {'feat'}, dimensions={0}, use_global_device_ids=true | all-gather | bytes 278528 | tf_op jit(solution)/shard_map/all_gather | solution.py:55
  266.8 4.6 %fusion.16 = f32[128]{0:T(128)S(1)} fusion(f32[512,2048]{1,0:T(8,128)} %param.7, f32[512,128]{1,0:T(8,128)S(1)} %all_gather.11), kind=kOutput, calls=%fused_computation.20 | convolution fusion | flops 1611202432 | bytes 4456960 | tf_op jit(solution)/shard_map/dot_general | solution.py:59
  271.4 29.8 %pmax.7 = f32[128]{0:T(128)S(1)} all-reduce(f32[128]{0:T(128)S(1)} %fusion.16), channel_id=1, replica_groups=mesh['groups'=2,'feat'=16] {'feat'}, use_global_device_ids=true, to_apply=%region_9.10 | all-reduce | flops 128 | bytes 1024 | tf_op jit(solution)/shard_map/pmax | solution.py:77
  (61 shorter events, 10.4 us)
Async XLA Ops:
  7.2 69.2 %reduce-scatter.10.cloned.1.call-start = ((), (), s32[]{:S(2)}) async-start(), calls=%async_computation.3 | async-start | bytes 278528
  10.3 7.4 %copy-start.3 = (s32[16]{0:T(128)S(1)}, s32[16]{0:T(128)}, u32[]{:S(2)}) copy-start(s32[16]{0:T(128)} %param.13) | copy-start | bytes 196
  10.4 7.4 %copy-start.5 = (s32[16]{0:T(128)S(1)}, s32[16]{0:T(128)}, u32[]{:S(2)}) copy-start(s32[16]{0:T(128)} %param.12) | copy-start | bytes 196
  10.4 13.0 %copy-start.2 = (f32[512,128]{1,0:T(8,128)S(1)}, f32[512,128]{1,0:T(8,128)}, u32[]{:S(2)}) copy-start(f32[512,128]{1,0:T(8,128)} %param.8) | copy-start | bytes 786436
  17.7 143.4 %reduce-scatter.12.cloned.1.call-start = ((), (), s32[]{:S(2)}) async-start(), calls=%async_computation.4 | async-start | bytes 278528
  17.9 98.7 %collective-permute-start = (s32[4]{0:T(128)S(1)}, s32[4]{0:T(128)S(1)}, u32[]{:S(2)}, u32[]{:S(2)}) collective-permute-start(s32[4]{0:T(128)S(1)} %get-tuple-element.16), channel_id=1, source_target_pairs={{0,1},{1,2},{2,3},{3,4},{4,5},{5,6},{6,7},{7,8},{8,9},{9,10},{10,1... | collective-permute-start | bytes 56 | tf_op jit(solution)/shard_map/ppermute | solution.py:17
  18.4 98.2 %collective-permute-start.1 = (s32[4]{0:T(128)S(1)}, s32[4]{0:T(128)S(1)}, u32[]{:S(2)}, u32[]{:S(2)}) collective-permute-start(s32[4]{0:T(128)S(1)} %get-tuple-element.17), channel_id=1, source_target_pairs={{0,15},{1,0},{2,1},{3,2},{4,3},{5,4},{6,5},{7,6},{8,7},{9,8},{10,9... | collective-permute-start | bytes 56 | tf_op jit(solution)/shard_map/ppermute | solution.py:17
  23.5 5.1 %copy-start.4 = (f32[128]{0:T(128)S(1)}, f32[128]{0:T(128)}, u32[]{:S(2)}) copy-start(f32[128]{0:T(128)} %param.11) | copy-start | bytes 1540
  77.2 25.4 %copy-start = (f32[512,2048]{1,0:T(8,128)S(1)}, f32[512,2048]{1,0:T(8,128)}, u32[]{:S(2)}) copy-start(f32[512,2048]{1,0:T(8,128)} %param.7) | copy-start | bytes 12582916
  108.0 137.7 %reduce-scatter.14.cloned.1.call-start = ((), (), s32[]{:S(2)}) async-start(), calls=%async_computation.5 | async-start | bytes 278528
  112.1 116.7 %collective-permute-start.4 = (f32[512,4,128]{2,1,0:T(4,128)}, f32[512,4,128]{2,1,0:T(4,128)}, u32[]{:S(2)}, u32[]{:S(2)}) collective-permute-start(f32[512,4,128]{2,1,0:T(4,128)} %get-tuple-element.12), channel_id=1, source_target_pairs={{0,1},{1,2},{2,3},{3,4},{4,5},{5,6},{6,7},{7,8},{8,9},{9,10},{10,1... | collective-permute-start | bytes 3145736 | tf_op jit(solution)/shard_map/ppermute | solution.py:17
  112.5 116.4 %collective-permute-start.5 = (f32[512,4,128]{2,1,0:T(4,128)}, f32[512,4,128]{2,1,0:T(4,128)}, u32[]{:S(2)}, u32[]{:S(2)}) collective-permute-start(f32[512,4,128]{2,1,0:T(4,128)} %get-tuple-element.13), channel_id=1, source_target_pairs={{0,15},{1,0},{2,1},{3,2},{4,3},{5,4},{6,5},{7,6},{8,7},{9,8},{10,9... | collective-permute-start | bytes 3145736 | tf_op jit(solution)/shard_map/ppermute | solution.py:17
  162.0 25.3 %copy-start.1 = (f32[512,2048]{1,0:T(8,128)S(1)}, f32[512,2048]{1,0:T(8,128)}, u32[]{:S(2)}) copy-start(f32[512,2048]{1,0:T(8,128)} %param.7) | copy-start | bytes 12582916
  193.0 46.0 %collective-permute-start.2 = (f32[4,128,128]{2,0,1:T(4,128)S(1)}, f32[4,128,128]{2,0,1:T(4,128)S(1)}, u32[]{:S(2)}, u32[]{:S(2)}) collective-permute-start(f32[4,128,128]{2,0,1:T(4,128)S(1)} %copy.41), channel_id=1, source_target_pairs={{0,1},{1,2},{2,3},{3,4},{4,5},{5,6},{6,7},{7,8},{8,9},{9,10},{10,1... | collective-permute-start | bytes 786440 | tf_op jit(solution)/shard_map/ppermute | solution.py:17
  193.6 45.4 %collective-permute-start.3 = (f32[4,128,128]{2,0,1:T(4,128)S(1)}, f32[4,128,128]{2,0,1:T(4,128)S(1)}, u32[]{:S(2)}, u32[]{:S(2)}) collective-permute-start(f32[4,128,128]{2,0,1:T(4,128)S(1)} %copy.42), channel_id=1, source_target_pairs={{0,15},{1,0},{2,1},{3,2},{4,3},{5,4},{6,5},{7,6},{8,7},{9,8},{10,9... | collective-permute-start | bytes 786440 | tf_op jit(solution)/shard_map/ppermute | solution.py:17
  228.9 72.5 %copy-start.6 = (f32[128]{0:T(128)}, f32[128]{0:T(128)S(1)}, u32[]{:S(2)}) copy-start(f32[128]{0:T(128)S(1)} %psum.7) | copy-start | bytes 1540
Sparse Core Ops, SparseCore 0:
  17.8 58.4 reduce-scatter.9
  108.1 52.9 reduce-scatter.11
  192.8 52.8 reduce-scatter.13
where the time goes:
time: 309 us; the launch traced here: 308 us
  blocking collectives  121 us (39%)
  waiting for transfers between devices  96.2 us (31%)
  matrix products  37.2 us (12%)
  local copies, waits for them, and re-layouts  24.4 us (8%)
  starting transfers between devices  14.8 us (5%)
  between operations  14 us (5%)
    unnamed x6, waiting for transfers between devices  96.2 us
    all_gather x3, blocking collectives, misfit_of(): lax.all_gather(fitted_rows - own_targets, 'feat', axis=0, tiled=True)  60.7 us
    psum x1, blocking collectives, local(): mass = lax.psum(local_mass, 'feat')  30.2 us
    pmax x1, blocking collectives, local(): peak = lax.pmax(local_peak, 'feat')  29.8 us
    unnamed x26, local copies, waits for them, and re-layouts  17.6 us
    dot_general x3, matrix products, misfit_of(): jnp.dot(design, point, precision=precise, preferred_element_type=jnp.floa...  15.4 us
    dot_general x3, matrix products, correlate(): lax.dot_general(design, misfit, (((0,), (0,)), ((), ())), precision=preci...  14.7 us
    ppermute x6, starting transfers between devices, shifted(): return lax.ppermute(value, axis, pairs)  14.5 us
  transfers between devices with their start and end apart: 9, of which 3 were waited for; matrix products, arithmetic and copies ran while one was open for 15% of the time, Pallas kernels for 0%

commit v1 on v0

v1 whole, which is shorter than its diff:
```python
import functools
import math

import jax
import jax.numpy as jnp
from jax import lax
from jax.experimental import pallas as pl
from jax.experimental.pallas import tpu as pltpu
from jax.sharding import PartitionSpec as P

START = 40
LANE = 128
AXIS = "feat"


def swap(value, bit):
    count = lax.axis_size(AXIS)
    return lax.ppermute(value, AXIS, [(i, i ^ bit) for i in range(count)])


def stages(count):
    return [1 << s for s in range(count.bit_length() - 1)]


def halves(values):
    high = values.astype(jnp.bfloat16)
    low = (values - high.astype(jnp.float32)).astype(jnp.bfloat16)
    return high, low


def mul(left, right):
    return lax.dot_general(left, right, (((1,), (0,)), ((), ())), preferred_element_type=jnp.float32)


def shrink(values, level):
    return values - jnp.clip(values, -level, level)


def forward(high, low, point):
    width = point.shape[1]
    ph, plo = halves(point)
    both = mul(high, jnp.concatenate([ph, plo], axis=1))
    return both[:, :width] + both[:, width:] + mul(low, ph)


def backward(high, low, turned):
    width = turned.shape[0] // 2
    both = mul(turned, high)
    return both[:width] + both[width:] + mul(turned[:width], low)


def hand_over(parity, total, keep_ref, send_ref):
    half = keep_ref.shape[0]
    keep_ref[...] = total[pl.ds(pl.multiple_of(parity * half, 8), half), :]
    send_ref[...] = total[pl.ds(pl.multiple_of((1 - parity) * half, 8), half), :]


def take_over(parity, own_ref, other_ref, targets_ref, turned, whole):
    half = own_ref.shape[0]
    whole[pl.ds(pl.multiple_of(parity * half, 8), half), :] = own_ref[...]
    whole[pl.ds(pl.multiple_of((1 - parity) * half, 8), half), :] = other_ref[...]
    width = targets_ref.shape[1]
    misfit = whole[...] - targets_ref[...]
    across = misfit.T
    high, low = halves(across)
    turned[:width] = high
    turned[width:] = low
    return misfit


def first_kernel(push, flags_ref, parity_ref, design_ref, now_ref, prev_ref, keep_ref, send_ref, near_ref, far_ref, total):
    step = pl.program_id(0)
    last = pl.num_programs(0) - 1
    parity = parity_ref[0]
    block = design_ref[...]
    high, low = halves(block)
    now = now_ref[...]
    part = forward(high, low, now + push * (now - prev_ref[...]))
    rows = block.shape[0]
    edge = block.shape[1] // LANE

    @pl.when(step == 0)
    def _():
        total[...] = part

    @pl.when(step > 0)
    def _():
        total[...] += part

    def put(ref, side):
        ref[:rows, :] = block
        for k in range(edge):
            flag = flags_ref[side * edge + k]
            ref[rows:, k * LANE : (k + 1) * LANE] = jnp.full((8, LANE), flag, jnp.float32)

    @pl.when((step == 0) & (parity == 1))
    def _():
        put(near_ref, 0)

    @pl.when((step == 0) & (parity == 0))
    def _():
        put(far_ref, 0)

    @pl.when((step == last) & (parity == 0))
    def _():
        put(near_ref, 1)

    @pl.when((step == last) & (parity == 1))
    def _():
        put(far_ref, 1)

    @pl.when(step == last)
    def _():
        hand_over(parity, total, keep_ref, send_ref)


def descend_kernel(
    push_in, push_out, scale, level_scale, parity_ref, design_ref, later_ref, early_ref, own_ref, other_ref, targets_ref,
    penalty_ref, coef_ref, keep_ref, send_ref, mass_ref, total, turned,
):
    step = pl.program_id(0)
    parity = parity_ref[0]

    @pl.when(step == 0)
    def _():
        take_over(parity, own_ref, other_ref, targets_ref, turned, total)

    high, low = halves(design_ref[...])
    turn = backward(high, low, turned[...])
    later = later_ref[...]
    point = later + push_in * (later - early_ref[...])
    coef = shrink(point - turn.T * (1.0 / scale), penalty_ref[...] * level_scale)
    coef_ref[...] = coef
    mass = jnp.sum(jnp.abs(coef), axis=0, keepdims=True)
    if push_out is not None:
        part = forward(high, low, coef + push_out * (coef - later))
    else:
        part = forward(high, low, coef)

    @pl.when(step == 0)
    def _():
        total[...] = part
        mass_ref[...] = jnp.broadcast_to(mass, mass_ref.shape)

    @pl.when(step > 0)
    def _():
        total[...] += part
        mass_ref[...] += jnp.broadcast_to(mass, mass_ref.shape)

    @pl.when(step == pl.num_programs(0) - 1)
    def _():
        hand_over(parity, total, keep_ref, send_ref)


def peak_kernel(parity_ref, design_ref, own_ref, other_ref, targets_ref, peak_ref, square_ref, cross_ref, total, turned, best):
    step = pl.program_id(0)
    parity = parity_ref[0]

    @pl.when(step == 0)
    def _():
        residual = -take_over(parity, own_ref, other_ref, targets_ref, turned, total)
        square_ref[...] = jnp.sum(residual * residual, axis=0, keepdims=True)
        cross_ref[...] = jnp.sum(residual * targets_ref[...], axis=0, keepdims=True)
        best[...] = jnp.zeros_like(best)

    high, low = halves(design_ref[...])
    turn = jnp.abs(backward(high, low, turned[...]))
    for k in range(turn.shape[1] // LANE):
        best[...] = jnp.maximum(best[...], turn[:, k * LANE : (k + 1) * LANE])

    @pl.when(step == pl.num_programs(0) - 1)
    def _():
        peak_ref[...] = jnp.broadcast_to(jnp.max(best[...].T, axis=0, keepdims=True), peak_ref.shape)


def place_kernel(edge, along, table_ref, parity_ref, near_ref, own_ref, far_ref, out_ref, blank, sems):
    slots = table_ref.shape[0]
    own = slots - 2 * edge
    parity = parity_ref[0]
    blank[...] = jnp.zeros_like(blank)

    def piece(ref, index):
        start = pl.multiple_of(index * LANE, LANE)
        if along == 1:
            return ref.at[0 : out_ref.shape[0], pl.ds(start, LANE)]
        return ref.at[pl.ds(start, LANE), :]

    def copy(slot, src):
        return pltpu.make_async_copy(src, piece(out_ref, slot), sems.at[slot])

    for slot in range(slots):
        source = table_ref[slot]
        left = (source >= 0) & (source < edge)
        right = source >= edge + own
        from_near = (left & (parity == 1)) | (right & (parity == 0))
        from_far = (left & (parity == 0)) | (right & (parity == 1))
        inner = jnp.where(left, source, source - edge - own)

        @pl.when(source < 0)
        def _():
            copy(slot, blank).start()

        @pl.when((source >= edge) & (source < edge + own))
        def _():
            copy(slot, piece(own_ref, source - edge)).start()

        @pl.when(from_near)
        def _():
            copy(slot, piece(near_ref, inner)).start()

        @pl.when(from_far)
        def _():
            copy(slot, piece(far_ref, inner)).start()

    for slot in range(slots):
        copy(slot, blank).wait()


VM = pltpu.MemorySpace.VMEM
SM = pltpu.MemorySpace.SMEM


def whole():
    return pl.BlockSpec(memory_space=VM)


def scalars():
    return pl.BlockSpec(memory_space=SM)


def f32(*shape):
    return jax.ShapeDtypeStruct(shape, jnp.float32)


def fixed(shape):
    return pl.BlockSpec(shape, lambda i: (0,) * len(shape))


def local(design, targets, coef_now, coef_prev, penalty, drop_mask, dest_shard):
    samples, feats = design.shape
    width = targets.shape[1]
    shards = lax.axis_size(AXIS)
    me = lax.axis_index(AXIS)
    parity = (me & 1).astype(jnp.int32).reshape(1)
    lipschitz = (math.sqrt(samples) + math.sqrt(feats * shards)) ** 2
    first_push = (START - 1) / (START + 2)
    second_push = START / (START + 3)
    blocks = feats // LANE
    edge = blocks // 4
    chunk = edge * LANE
    steps = feats // chunk
    half = samples // 2

    survive = drop_mask == 0
    to_left = survive[:edge] & (dest_shard[:edge] == (me + shards - 1) % shards)
    to_right = survive[blocks - edge :] & (dest_shard[blocks - edge :] == (me + 1) % shards)
    staying = survive & (dest_shard == me)
    flags = jnp.concatenate([to_left, to_right]).astype(jnp.float32)

    def feat_spec():
        return pl.BlockSpec((samples, chunk), lambda i: (0, i))

    def coef_spec():
        return pl.BlockSpec((chunk, width), lambda i: (i, 0))

    params = pltpu.CompilerParams(vmem_limit_bytes=24 << 20, dimension_semantics=("arbitrary",))
    row_spec = fixed((1, width))
    half_spec = fixed((half, width))

    keep, send, near, far = pl.pallas_call(
        functools.partial(first_kernel, first_push),
        grid=(steps,),
        in_specs=[scalars(), scalars(), feat_spec(), coef_spec(), coef_spec()],
        out_specs=[half_spec, half_spec, fixed((samples + 8, chunk)), fixed((samples + 8, chunk))],
        out_shape=[f32(half, width)] * 2 + [f32(samples + 8, chunk)] * 2,
        scratch_shapes=[pltpu.VMEM((samples, width), jnp.float32)],
        compiler_params=params,
        name="first",
    )(flags, parity, design, coef_now, coef_prev)

    def outward(value):
        count = lax.axis_size(AXIS)
        pairs = [(i, (i + 1) % count if i % 2 else (i - 1) % count) for i in range(count)]
        return lax.ppermute(value, AXIS, pairs)

    def combine(keep, send, rows):
        total = keep + swap(send, 1)
        for bit in stages(shards)[1:]:
            total = total + swap(total, bit)
        other = swap(total[:rows], 1)
        return total, other

    near_in = swap(near, 1)
    far_in = outward(far)

    turned = pltpu.VMEM((2 * width, samples), jnp.bfloat16)
    sum_scratch = pltpu.VMEM((samples, width), jnp.float32)

    def descend(push_in, push_out, later, early, own, other):
        return pl.pallas_call(
            functools.partial(descend_kernel, push_in, push_out, lipschitz, samples / lipschitz),
            grid=(steps,),
            in_specs=[scalars(), feat_spec(), coef_spec(), coef_spec(), half_spec, half_spec, fixed((samples, width)), row_spec],
            out_specs=[coef_spec(), half_spec, half_spec, fixed((8, width))],
            out_shape=[f32(feats, width), f32(half, width), f32(half, width), f32(8, width)],
            scratch_shapes=[sum_scratch, turned],
            compiler_params=params,
            name="descend",
        )(parity, design, later, early, own, other, targets, penalty.reshape(1, width))

    own, other = combine(keep, send, half)
    coef_one, keep, send, _ = descend(first_push, second_push, coef_now, coef_prev, own, other)
    own, other = combine(keep, send, half)
    coef_two, keep, send, mass = descend(second_push, None, coef_one, coef_now, own, other)

    odd = (me & 1) == 1
    left_edge, right_edge = coef_two[:chunk], coef_two[feats - chunk :]
    near_coef = swap(jnp.where(odd, left_edge, right_edge), 1)
    far_coef = outward(jnp.where(odd, right_edge, left_edge))

    own, other = combine(jnp.concatenate([keep, mass]), jnp.concatenate([send, mass]), half)
    mass = own[half]
    own = own[:half]
    peak, square, cross = pl.pallas_call(
        peak_kernel,
        grid=(steps,),
        in_specs=[scalars(), feat_spec(), half_spec, half_spec, fixed((samples, width))],
        out_specs=[fixed((8, width)), row_spec, row_spec],
        out_shape=[f32(8, width), f32(1, width), f32(1, width)],
        scratch_shapes=[sum_scratch, turned, pltpu.VMEM((width, LANE), jnp.float32)],
        compiler_params=params,
        name="peak",
    )(parity, design, own, other, targets)
    for bit in stages(shards):
        peak = jnp.maximum(peak, swap(peak, bit))

    dual_scale = jnp.maximum(penalty, peak[0] / samples)
    ratio = penalty / dual_scale
    dual_value = (2.0 * ratio * cross[0] - ratio * ratio * square[0]) / (2.0 * samples)
    duality_gap = square[0] / (2.0 * samples) + penalty * mass - dual_value

    near_flags = near_in[samples, ::LANE] > 0.5
    far_flags = far_in[samples, ::LANE] > 0.5
    before = jnp.where(odd, near_flags, far_flags)
    after = jnp.where(odd, far_flags, near_flags)
    arrived = jnp.concatenate([before, staying, after]).astype(jnp.int32)
    slots = blocks + 2 * edge
    slot_of = jnp.cumsum(arrived, dtype=jnp.int32) - 1
    ids = jnp.arange(slots, dtype=jnp.int32)
    hit = (slot_of[:, None] == ids[None, :]) & (arrived[:, None] > 0)
    table = jnp.sum(jnp.where(hit, ids[:, None] + 1, 0), axis=0) - 1

    def place(along, near_part, own_part, far_part, out):
        block = (samples, LANE) if along == 1 else (LANE, width)
        return pl.pallas_call(
            functools.partial(place_kernel, edge, along),
            in_specs=[scalars(), scalars(), whole(), whole(), whole()],
            out_specs=pl.BlockSpec(memory_space=pl.ANY),
            out_shape=out,
            scratch_shapes=[pltpu.VMEM(block, jnp.float32), pltpu.SemaphoreType.DMA((slots,))],
            compiler_params=pltpu.CompilerParams(vmem_limit_bytes=24 << 20),
            name="place",
        )(table, parity, near_part, own_part, far_part)

    design_out = place(1, near_in, design, far_in, f32(samples, slots * LANE))
    coef_out = place(0, near_coef, coef_two, far_coef, f32(slots * LANE, width))
    return (coef_out, design_out, duality_gap, dual_value, mass)


def solution(mesh):
    placed = (
        P("groups", "feat"),
        P("groups", None),
        P(("groups", "feat"), None),
        P(("groups", "feat"), None),
        P("groups"),
        P(("groups", "feat")),
        P(("groups", "feat")),
    )
    return jax.shard_map(
        local,
        mesh=mesh,
        in_specs=placed,
        out_specs=(
            P(("groups", "feat"), None),
            P("groups", "feat"),
            P("groups"),
            P("groups"),
            P("groups"),
        ),
        check_vma=False,
    )
```

time: 309 us -> 122 us (0.39)
  blocking collectives: 121 us -> 0 us
  matrix products: 37.2 us -> 0 us
  waiting for transfers between devices: 96.2 us -> 59.4 us
  Pallas kernels: 0 us -> 21.7 us
  local copies, waits for them, and re-layouts: 24.4 us -> 8.42 us
  between operations: 14 us -> 0.85 us
  starting transfers between devices: 14.8 us -> 26.6 us
  other arithmetic: 0.99 us -> 5.07 us
    unnamed x6 -> x0, waiting for transfers between devices: 96.2 us -> none
    all_gather x3 -> x0, blocking collectives: 60.7 us -> none  [misfit_of(): lax.all_gather(fitted_rows - own_targets, 'feat', axis=0, tiled=True)]
    ppermute x6 -> x23, waiting for transfers between devices: 0.02 us -> 59.4 us  [the longest x21 59.4 us: swap(): return lax.ppermute(value, AXIS, [(i, i ^ bit) for i in range(count)])]
    dot_general x8 -> x0, matrix products: 37.2 us -> none  [the longest x3 15.4 us: misfit_of(): jnp.dot(design, point, precision=precise, preferred_element_type=jnp.floa...]
    psum x1 -> x0, blocking collectives: 30.2 us -> none  [local(): mass = lax.psum(local_mass, 'feat')]
    pmax x1 -> x0, blocking collectives: 29.8 us -> none  [local(): peak = lax.pmax(local_peak, 'feat')]
    pallas_call x0 -> x6, Pallas kernels: none -> 21.7 us  [the longest x2 9.08 us: descend(): pl.pallas_call(functools.partial(descend_kernel, push_in, push_out, lipsc...]
    ppermute x6 -> x23, starting transfers between devices: 14.5 us -> 26.6 us  [the longest x21 18.6 us: swap(): return lax.ppermute(value, AXIS, [(i, i ^ bit) for i in range(count)])]
  transfers between devices with their start and end apart: 9 -> 23, of which waited for: 3 -> 17; matrix products, arithmetic and copies ran while one was open for 15% -> 1% of each run, Pallas kernels for 0% -> 8%
where the time goes in v1:
time: 122 us
  waiting for transfers between devices  59.4 us (49%)
  starting transfers between devices  26.6 us (22%)
  Pallas kernels  21.7 us (18%)
  local copies, waits for them, and re-layouts  8.42 us (7%)
  other arithmetic  5.07 us (4%)
    ppermute x21, waiting for transfers between devices, swap(): return lax.ppermute(value, AXIS, [(i, i ^ bit) for i in range(count)])  59.4 us
    ppermute x21, starting transfers between devices, swap(): return lax.ppermute(value, AXIS, [(i, i ^ bit) for i in range(count)])  18.6 us
    pallas_call x2, Pallas kernels, descend(): pl.pallas_call(functools.partial(descend_kernel, push_in, push_out, lipsc...  9.08 us
    ppermute x2, starting transfers between devices, outward(): return lax.ppermute(value, AXIS, pairs)  8.03 us
    unnamed x20, local copies, waits for them, and re-layouts  7.49 us
    pallas_call x2, Pallas kernels, place(): pl.pallas_call(functools.partial(place_kernel, edge, along), in_specs=[sc...  5.27 us
    pallas_call x1, Pallas kernels, local(): pl.pallas_call(functools.partial(first_kernel, first_push), grid=(steps,)...  4.3 us
    pallas_call x1, Pallas kernels, local(): pl.pallas_call(peak_kernel, grid=(steps,), in_specs=[scalars(), feat_spec...  3.03 us
  transfers between devices with their start and end apart: 23, of which 17 were waited for; matrix products, arithmetic and copies ran while one was open for 1% of the time, Pallas kernels for 8%

profile of v1, /device:TPU:0, one launch (start us, length us, event | category | flops | bytes accessed | tf_op | source)
XLA Modules:
  0.0 122.1 jit_solution(8929152081934600765)
XLA Ops:
  2.2 2.2 %copy-done = f32[512,2048]{1,0:T(8,128)S(1)} copy-done((f32[512,2048]{1,0:T(8,128)S(1)}, f32[512,2048]{1,0:T(8,128)}, u32[]{:S(2)}) %copy-start) | copy-done | bytes 4194328
  6.9 4.3 %first.1 = (f32[256,128]{1,0:T(8,128)S(1)}, f32[256,128]{1,0:T(8,128)S(1)}, f32[520,512]{1,0:T(8,128)}, f32[520,512]{1,0:T(8,128)}) custom-call(f32[8]{0:T(128)S(1)} %add_convert_fusion.flags_ref, s32[1]{0:T(128)} %bitcast.parity_ref, f32[512,2048]{1,0:T(8,128)S(1)} %copy-done, f32[2048,128]{1,0:T(8,128)S(1)} %copy-done.3, f32[2048,128]{1,0:T(8,128)S(1)} %copy-done.5), custom_call_target="tpu_custom_call" | custom-call | tf_op jit(solution)/shard_map/first/pallas_call | solution.py:270
  12.7 2.9 %collective-permute-start.3 = (f32[256,128]{1,0:T(8,128)S(1)}, f32[256,128]{1,0:T(8,128)S(1)}, u32[]{:S(2)}, u32[]{:S(2)}) collective-permute-start(f32[256,128]{1,0:T(8,128)S(1)} %add.72), channel_id=1, source_target_pairs={{0,2},{1,3},{2,0},{3,1},{4,6},{5,7},{6,4},{7,5},{8,10},{9,11},{10,... | collective-permute-start | bytes 393224 | tf_op jit(solution)/shard_map/ppermute | solution.py:18
  15.6 3.8 %collective-permute-done.3 = f32[256,128]{1,0:T(8,128)S(1)} collective-permute-done((f32[256,128]{1,0:T(8,128)S(1)}, f32[256,128]{1,0:T(8,128)S(1)}, u32[]{:S(2)}, u32[]{:S(2)}) %collective-permute-start.3) | collective-permute-done | bytes 131104 | tf_op jit(solution)/shard_map/ppermute | solution.py:18
  19.4 1.9 %collective-permute-start.4 = (f32[256,128]{1,0:T(8,128)S(1)}, f32[256,128]{1,0:T(8,128)S(1)}, u32[]{:S(2)}, u32[]{:S(2)}) collective-permute-start(f32[256,128]{1,0:T(8,128)S(1)} %add.73), channel_id=1, source_target_pairs={{0,4},{1,5},{2,6},{3,7},{4,0},{5,1},{6,2},{7,3},{8,12},{9,13},{10,... | collective-permute-start | bytes 393224 | tf_op jit(solution)/shard_map/ppermute | solution.py:18
  21.3 3.2 %collective-permute-done.4 = f32[256,128]{1,0:T(8,128)S(1)} collective-permute-done((f32[256,128]{1,0:T(8,128)S(1)}, f32[256,128]{1,0:T(8,128)S(1)}, u32[]{:S(2)}, u32[]{:S(2)}) %collective-permute-start.4) | collective-permute-done | bytes 131104 | tf_op jit(solution)/shard_map/ppermute | solution.py:18
  24.5 2.9 %collective-permute-start.5 = (f32[256,128]{1,0:T(8,128)S(1)}, f32[256,128]{1,0:T(8,128)S(1)}, u32[]{:S(2)}, u32[]{:S(2)}) collective-permute-start(f32[256,128]{1,0:T(8,128)S(1)} %add.74), channel_id=1, source_target_pairs={{0,8},{1,9},{2,10},{3,11},{4,12},{5,13},{6,14},{7,15},{8,0},{9,1},... | collective-permute-start | bytes 393224 | tf_op jit(solution)/shard_map/ppermute | solution.py:18
  27.4 5.0 %collective-permute-done.5 = f32[256,128]{1,0:T(8,128)S(1)} collective-permute-done((f32[256,128]{1,0:T(8,128)S(1)}, f32[256,128]{1,0:T(8,128)S(1)}, u32[]{:S(2)}, u32[]{:S(2)}) %collective-permute-start.5) | collective-permute-done | bytes 131104 | tf_op jit(solution)/shard_map/ppermute | solution.py:18
  33.8 4.9 %descend.2 = (f32[2048,128]{1,0:T(8,128)S(1)}, f32[256,128]{1,0:T(8,128)S(1)}, f32[256,128]{1,0:T(8,128)S(1)}, f32[8,128]{1,0:T(8,128)}) custom-call(s32[1]{0:T(128)} %bitcast.parity_ref, f32[512,2048]{1,0:T(8,128)S(1)} %copy-done.1, f32[2048,128]{1,0:T(8,128)S(1)} %copy-done.4, f32[2048,128]{1,0:T(8,128)S(1)} %copy-done.6, f32[256,128]{1,0:T(8,128)S(1)} %add.75.own_ref, ...), custom_call_target="tpu_custom_call" | custom-call | tf_op jit(solution)/shard_map/descend/pallas_call | solution.py:300
  41.3 4.4 %collective-permute-done.8 = f32[256,128]{1,0:T(8,128)S(1)} collective-permute-done((f32[256,128]{1,0:T(8,128)S(1)}, f32[256,128]{1,0:T(8,128)S(1)}, u32[]{:S(2)}, u32[]{:S(2)}) %collective-permute-start.8) | collective-permute-done | bytes 131104 | tf_op jit(solution)/shard_map/ppermute | solution.py:18
  46.1 4.0 %collective-permute-start.1 = (f32[520,512]{1,0:T(8,128)}, f32[520,512]{1,0:T(8,128)S(1)}, u32[]{:S(2)}, u32[]{:S(2)}) collective-permute-start(f32[520,512]{1,0:T(8,128)} %get-tuple-element.20), channel_id=1, source_target_pairs={{0,15},{1,2},{2,1},{3,4},{4,3},{5,6},{6,5},{7,8},{8,7},{9,10},{10,... | collective-permute-start | bytes 3194888 | tf_op jit(solution)/shard_map/ppermute | solution.py:284
  50.8 1.8 %collective-permute-start.10 = (f32[256,128]{1,0:T(8,128)S(1)}, f32[256,128]{1,0:T(8,128)S(1)}, u32[]{:S(2)}, u32[]{:S(2)}) collective-permute-start(f32[256,128]{1,0:T(8,128)S(1)} %add.78), channel_id=1, source_target_pairs={{0,8},{1,9},{2,10},{3,11},{4,12},{5,13},{6,14},{7,15},{8,0},{9,1},... | collective-permute-start | bytes 393224 | tf_op jit(solution)/shard_map/ppermute | solution.py:18
  52.5 16.3 %collective-permute-done.10 = f32[256,128]{1,0:T(8,128)S(1)} collective-permute-done((f32[256,128]{1,0:T(8,128)S(1)}, f32[256,128]{1,0:T(8,128)S(1)}, u32[]{:S(2)}, u32[]{:S(2)}) %collective-permute-start.10) | collective-permute-done | bytes 131104 | tf_op jit(solution)/shard_map/ppermute | solution.py:18
  70.3 4.2 %descend.3 = (f32[2048,128]{1,0:T(8,128)S(1)}, f32[256,128]{1,0:T(8,128)S(1)}, f32[256,128]{1,0:T(8,128)S(1)}, f32[8,128]{1,0:T(8,128)S(1)}) custom-call(s32[1]{0:T(128)} %bitcast.parity_ref, f32[512,2048]{1,0:T(8,128)S(1)} %copy-done.1, f32[2048,128]{1,0:T(8,128)S(1)} %get-tuple-element.23.later_ref, f32[2048,128]{1,0:T(8,128)S(1)} %copy-done.4, ...), custom_call_target="tpu_custom_call" | custom-call | tf_op jit(solution)/shard_map/descend/pallas_call | solution.py:300
  77.3 4.3 %collective-permute-done.15 = f32[264,128]{1,0:T(8,128)S(1)} collective-permute-done((f32[264,128]{1,0:T(8,128)S(1)}, f32[264,128]{1,0:T(8,128)S(1)}, u32[]{:S(2)}, u32[]{:S(2)}) %collective-permute-start.15) | collective-permute-done | bytes 135200 | tf_op jit(solution)/shard_map/ppermute | solution.py:18
  83.5 4.1 %collective-permute-done.16 = f32[264,128]{1,0:T(8,128)} collective-permute-done((f32[264,128]{1,0:T(8,128)}, f32[264,128]{1,0:T(8,128)}, u32[]{:S(2)}, u32[]{:S(2)}) %collective-permute-start.16) | collective-permute-done | bytes 135200 | tf_op jit(solution)/shard_map/ppermute | solution.py:18
  88.6 2.5 %collective-permute-start.17 = (f32[264,128]{1,0:T(8,128)S(1)}, f32[264,128]{1,0:T(8,128)S(1)}, u32[]{:S(2)}, u32[]{:S(2)}) collective-permute-start(f32[264,128]{1,0:T(8,128)S(1)} %add.82), channel_id=1, source_target_pairs={{0,8},{1,9},{2,10},{3,11},{4,12},{5,13},{6,14},{7,15},{8,0},{9,1},... | collective-permute-start | bytes 405512 | tf_op jit(solution)/shard_map/ppermute | solution.py:18
  91.1 5.4 %collective-permute-done.17 = f32[264,128]{1,0:T(8,128)S(1)} collective-permute-done((f32[264,128]{1,0:T(8,128)S(1)}, f32[264,128]{1,0:T(8,128)S(1)}, u32[]{:S(2)}, u32[]{:S(2)}) %collective-permute-start.17) | collective-permute-done | bytes 135200 | tf_op jit(solution)/shard_map/ppermute | solution.py:18
  99.5 2.2 %copy-done.2 = f32[512,2048]{1,0:T(8,128)S(1)} copy-done((f32[512,2048]{1,0:T(8,128)S(1)}, f32[512,2048]{1,0:T(8,128)}, u32[]{:S(2)}) %copy-start.2) | copy-done | bytes 4194328
  101.7 3.0 %peak.1 = (f32[8,128]{1,0:T(8,128)S(1)}, f32[1,128]{1,0:T(1,128)S(1)}, f32[1,128]{1,0:T(1,128)S(1)}) custom-call(s32[1]{0:T(128)} %bitcast.parity_ref, f32[512,2048]{1,0:T(8,128)S(1)} %copy-done.2, f32[256,128]{1,0:T(8,128)} %slice.45.own_ref, f32[256,128]{1,0:T(8,128)} %collective-permute-done.18.other_ref, f32[512,128]{1,0:T(8,128)S(1)} %copy-done.7), custom_call_target="tpu_custom_call" | custom-call | tf_op jit(solution)/shard_map/peak/pallas_call | solution.py:324
  107.1 4.1 %collective-permute-start.13 = (f32[512,128]{1,0:T(8,128)S(1)}, f32[512,128]{1,0:T(8,128)S(1)}, u32[]{:S(2)}, u32[]{:S(2)}) collective-permute-start(f32[512,128]{1,0:T(8,128)S(1)} %get-tuple-element.36), channel_id=1, source_target_pairs={{0,15},{1,2},{2,1},{3,4},{4,3},{5,6},{6,5},{7,8},{8,7},{9,10},{10,... | collective-permute-start | bytes 786440 | tf_op jit(solution)/shard_map/ppermute | solution.py:284
  111.2 3.9 %collective-permute-done.21 = f32[8,128]{1,0:T(8,128)S(1)} collective-permute-done((f32[8,128]{1,0:T(8,128)S(1)}, f32[8,128]{1,0:T(8,128)S(1)}, u32[]{:S(2)}, u32[]{:S(2)}) %collective-permute-start.21) | collective-permute-done | bytes 4128 | tf_op jit(solution)/shard_map/ppermute | solution.py:18
  115.5 3.4 %place.3 = f32[512,3072]{1,0:T(8,128)} custom-call(s32[24]{0:T(128)S(1)} %broadcast_add_fusion.table_ref, s32[1]{0:T(128)} %bitcast.parity_ref, f32[520,512]{1,0:T(8,128)S(1)} %collective-permute-done.near_ref, f32[512,2048]{1,0:T(8,128)S(1)} %copy-done.2, f32[520,512]{1,0:T(8,128)S(1)} %collective-permute-done.1.far_ref), custom_call_target="tpu_custom_call" | custom-call | tf_op jit(solution)/shard_map/place/pallas_call | solution.py:355
  119.0 1.9 %place.2 = f32[3072,128]{1,0:T(8,128)} custom-call(s32[24]{0:T(128)S(1)} %broadcast_add_fusion.table_ref, s32[1]{0:T(128)} %bitcast.parity_ref, f32[512,128]{1,0:T(8,128)S(1)} %collective-permute-done.12.near_ref, f32[2048,128]{1,0:T(8,128)S(1)} %get-tuple-element.26.own_ref, f32[512,128]{1,0:T(8,128)S(1)} %collective-permute-done.13.far_ref), custom_call_target="tpu_custom_call" | custom-call | tf_op jit(solution)/shard_map/place/pallas_call | solution.py:355
  (82 shorter events, 24.9 us)
Async XLA Ops:
  6.9 27.0 %copy-start.6 = (f32[2048,128]{1,0:T(8,128)S(1)}, f32[2048,128]{1,0:T(8,128)}, u32[]{:S(2)}) copy-start(f32[2048,128]{1,0:T(8,128)} %early_ref.2) | copy-start | bytes 3145732
  11.2 1.5 %collective-permute-start.2 = (f32[256,128]{1,0:T(8,128)S(1)}, f32[256,128]{1,0:T(8,128)S(1)}, u32[]{:S(2)}, u32[]{:S(2)}) collective-permute-start(f32[256,128]{1,0:T(8,128)S(1)} %get-tuple-element.22), channel_id=1, source_target_pairs={{0,1},{1,0},{2,3},{3,2},{4,5},{5,4},{6,7},{7,6},{8,9},{9,8},{10,11... | collective-permute-start | bytes 393224 | tf_op jit(solution)/shard_map/ppermute | solution.py:18
  12.7 6.7 %collective-permute-start.3 = (f32[256,128]{1,0:T(8,128)S(1)}, f32[256,128]{1,0:T(8,128)S(1)}, u32[]{:S(2)}, u32[]{:S(2)}) collective-permute-start(f32[256,128]{1,0:T(8,128)S(1)} %add.72), channel_id=1, source_target_pairs={{0,2},{1,3},{2,0},{3,1},{4,6},{5,7},{6,4},{7,5},{8,10},{9,11},{10,... | collective-permute-start | bytes 393224 | tf_op jit(solution)/shard_map/ppermute | solution.py:18
  19.4 5.0 %collective-permute-start.4 = (f32[256,128]{1,0:T(8,128)S(1)}, f32[256,128]{1,0:T(8,128)S(1)}, u32[]{:S(2)}, u32[]{:S(2)}) collective-permute-start(f32[256,128]{1,0:T(8,128)S(1)} %add.73), channel_id=1, source_target_pairs={{0,4},{1,5},{2,6},{3,7},{4,0},{5,1},{6,2},{7,3},{8,12},{9,13},{10,... | collective-permute-start | bytes 393224 | tf_op jit(solution)/shard_map/ppermute | solution.py:18
  24.5 7.9 %collective-permute-start.5 = (f32[256,128]{1,0:T(8,128)S(1)}, f32[256,128]{1,0:T(8,128)S(1)}, u32[]{:S(2)}, u32[]{:S(2)}) collective-permute-start(f32[256,128]{1,0:T(8,128)S(1)} %add.74), channel_id=1, source_target_pairs={{0,8},{1,9},{2,10},{3,11},{4,12},{5,13},{6,14},{7,15},{8,0},{9,1},... | collective-permute-start | bytes 393224 | tf_op jit(solution)/shard_map/ppermute | solution.py:18
  32.4 1.4 %collective-permute-start.6 = (f32[256,128]{1,0:T(8,128)S(1)}, f32[256,128]{1,0:T(8,128)S(1)}, u32[]{:S(2)}, u32[]{:S(2)}) collective-permute-start(f32[256,128]{1,0:T(8,128)S(1)} %add.75.own_ref), channel_id=1, source_target_pairs={{0,1},{1,0},{2,3},{3,2},{4,5},{5,4},{6,7},{7,6},{8,9},{9,8},{10,11... | collective-permute-start | bytes 393224 | tf_op jit(solution)/shard_map/ppermute | solution.py:18
  38.7 1.3 %collective-permute-start.7 = (f32[256,128]{1,0:T(8,128)S(1)}, f32[256,128]{1,0:T(8,128)S(1)}, u32[]{:S(2)}, u32[]{:S(2)}) collective-permute-start(f32[256,128]{1,0:T(8,128)S(1)} %get-tuple-element.25), channel_id=1, source_target_pairs={{0,1},{1,0},{2,3},{3,2},{4,5},{5,4},{6,7},{7,6},{8,9},{9,8},{10,11... | collective-permute-start | bytes 393224 | tf_op jit(solution)/shard_map/ppermute | solution.py:18
  40.1 5.6 %collective-permute-start.8 = (f32[256,128]{1,0:T(8,128)S(1)}, f32[256,128]{1,0:T(8,128)S(1)}, u32[]{:S(2)}, u32[]{:S(2)}) collective-permute-start(f32[256,128]{1,0:T(8,128)S(1)} %add.76), channel_id=1, source_target_pairs={{0,2},{1,3},{2,0},{3,1},{4,6},{5,7},{6,4},{7,5},{8,10},{9,11},{10,... | collective-permute-start | bytes 393224 | tf_op jit(solution)/shard_map/ppermute | solution.py:18
  45.7 5.0 %collective-permute-start.9 = (f32[256,128]{1,0:T(8,128)S(1)}, f32[256,128]{1,0:T(8,128)S(1)}, u32[]{:S(2)}, u32[]{:S(2)}) collective-permute-start(f32[256,128]{1,0:T(8,128)S(1)} %add.77), channel_id=1, source_target_pairs={{0,4},{1,5},{2,6},{3,7},{4,0},{5,1},{6,2},{7,3},{8,12},{9,13},{10,... | collective-permute-start | bytes 393224 | tf_op jit(solution)/shard_map/ppermute | solution.py:18
  46.1 37.2 %collective-permute-start = (f32[520,512]{1,0:T(8,128)}, f32[520,512]{1,0:T(8,128)S(1)}, u32[]{:S(2)}, u32[]{:S(2)}) collective-permute-start(f32[520,512]{1,0:T(8,128)} %get-tuple-element.19), channel_id=1, source_target_pairs={{0,1},{1,0},{2,3},{3,2},{4,5},{5,4},{6,7},{7,6},{8,9},{9,8},{10,11... | collective-permute-start | bytes 3194888 | tf_op jit(solution)/shard_map/ppermute | solution.py:18
  46.1 37.3 %collective-permute-start.1 = (f32[520,512]{1,0:T(8,128)}, f32[520,512]{1,0:T(8,128)S(1)}, u32[]{:S(2)}, u32[]{:S(2)}) collective-permute-start(f32[520,512]{1,0:T(8,128)} %get-tuple-element.20), channel_id=1, source_target_pairs={{0,15},{1,2},{2,1},{3,4},{4,3},{5,6},{6,5},{7,8},{8,7},{9,10},{10,... | collective-permute-start | bytes 3194888 | tf_op jit(solution)/shard_map/ppermute | solution.py:284
  50.8 18.0 %collective-permute-start.10 = (f32[256,128]{1,0:T(8,128)S(1)}, f32[256,128]{1,0:T(8,128)S(1)}, u32[]{:S(2)}, u32[]{:S(2)}) collective-permute-start(f32[256,128]{1,0:T(8,128)S(1)} %add.78), channel_id=1, source_target_pairs={{0,8},{1,9},{2,10},{3,11},{4,12},{5,13},{6,14},{7,15},{8,0},{9,1},... | collective-permute-start | bytes 393224 | tf_op jit(solution)/shard_map/ppermute | solution.py:18
  68.8 1.4 %collective-permute-start.11 = (f32[256,128]{1,0:T(8,128)S(1)}, f32[256,128]{1,0:T(8,128)S(1)}, u32[]{:S(2)}, u32[]{:S(2)}) collective-permute-start(f32[256,128]{1,0:T(8,128)S(1)} %add.79.own_ref), channel_id=1, source_target_pairs={{0,1},{1,0},{2,3},{3,2},{4,5},{5,4},{6,7},{7,6},{8,9},{9,8},{10,11... | collective-permute-start | bytes 393224 | tf_op jit(solution)/shard_map/ppermute | solution.py:18
  74.5 1.4 %collective-permute-start.14 = (f32[264,128]{1,0:T(8,128)S(1)}, f32[264,128]{1,0:T(8,128)S(1)}, u32[]{:S(2)}, u32[]{:S(2)}) collective-permute-start(f32[264,128]{1,0:T(8,128)S(1)} %pad_maximum_fusion), channel_id=1, source_target_pairs={{0,1},{1,0},{2,3},{3,2},{4,5},{5,4},{6,7},{7,6},{8,9},{9,8},{10,11... | collective-permute-start | bytes 405512 | tf_op jit(solution)/shard_map/ppermute | solution.py:18
  75.9 5.7 %collective-permute-start.15 = (f32[264,128]{1,0:T(8,128)S(1)}, f32[264,128]{1,0:T(8,128)S(1)}, u32[]{:S(2)}, u32[]{:S(2)}) collective-permute-start(f32[264,128]{1,0:T(8,128)S(1)} %fusion), channel_id=1, source_target_pairs={{0,2},{1,3},{2,0},{3,1},{4,6},{5,7},{6,4},{7,5},{8,10},{9,11},{10,... | collective-permute-start | bytes 405512 | tf_op jit(solution)/shard_map/ppermute | solution.py:18
  82.3 5.3 %collective-permute-start.16 = (f32[264,128]{1,0:T(8,128)}, f32[264,128]{1,0:T(8,128)}, u32[]{:S(2)}, u32[]{:S(2)}) collective-permute-start(f32[264,128]{1,0:T(8,128)} %add.81), channel_id=1, source_target_pairs={{0,4},{1,5},{2,6},{3,7},{4,0},{5,1},{6,2},{7,3},{8,12},{9,13},{10,... | collective-permute-start | bytes 405512 | tf_op jit(solution)/shard_map/ppermute | solution.py:18
  88.6 7.9 %collective-permute-start.17 = (f32[264,128]{1,0:T(8,128)S(1)}, f32[264,128]{1,0:T(8,128)S(1)}, u32[]{:S(2)}, u32[]{:S(2)}) collective-permute-start(f32[264,128]{1,0:T(8,128)S(1)} %add.82), channel_id=1, source_target_pairs={{0,8},{1,9},{2,10},{3,11},{4,12},{5,13},{6,14},{7,15},{8,0},{9,1},... | collective-permute-start | bytes 405512 | tf_op jit(solution)/shard_map/ppermute | solution.py:18
  97.8 1.7 %collective-permute-start.18 = (f32[256,128]{1,0:T(8,128)}, f32[256,128]{1,0:T(8,128)}, u32[]{:S(2)}, u32[]{:S(2)}) collective-permute-start(f32[256,128]{1,0:T(8,128)} %slice.45.own_ref), channel_id=1, source_target_pairs={{0,1},{1,0},{2,3},{3,2},{4,5},{5,4},{6,7},{7,6},{8,9},{9,8},{10,11... | collective-permute-start | bytes 393224 | tf_op jit(solution)/shard_map/ppermute | solution.py:18
  104.7 1.2 %collective-permute-start.19 = (f32[8,128]{1,0:T(8,128)S(1)}, f32[8,128]{1,0:T(8,128)S(1)}, u32[]{:S(2)}, u32[]{:S(2)}) collective-permute-start(f32[8,128]{1,0:T(8,128)S(1)} %get-tuple-element.31), channel_id=1, source_target_pairs={{0,1},{1,0},{2,3},{3,2},{4,5},{5,4},{6,7},{7,6},{8,9},{9,8},{10,11... | collective-permute-start | bytes 12296 | tf_op jit(solution)/shard_map/ppermute | solution.py:18
  106.0 5.2 %collective-permute-start.20 = (f32[8,128]{1,0:T(8,128)S(1)}, f32[8,128]{1,0:T(8,128)S(1)}, u32[]{:S(2)}, u32[]{:S(2)}) collective-permute-start(f32[8,128]{1,0:T(8,128)S(1)} %max.15), channel_id=1, source_target_pairs={{0,2},{1,3},{2,0},{3,1},{4,6},{5,7},{6,4},{7,5},{8,10},{9,11},{10,... | collective-permute-start | bytes 12296 | tf_op jit(solution)/shard_map/ppermute | solution.py:18
  107.0 12.0 %collective-permute-start.12 = (f32[512,128]{1,0:T(8,128)S(1)}, f32[512,128]{1,0:T(8,128)S(1)}, u32[]{:S(2)}, u32[]{:S(2)}) collective-permute-start(f32[512,128]{1,0:T(8,128)S(1)} %get-tuple-element.37), channel_id=1, source_target_pairs={{0,1},{1,0},{2,3},{3,2},{4,5},{5,4},{6,7},{7,6},{8,9},{9,8},{10,11... | collective-permute-start | bytes 786440 | tf_op jit(solution)/shard_map/ppermute | solution.py:18
  107.1 11.9 %collective-permute-start.13 = (f32[512,128]{1,0:T(8,128)S(1)}, f32[512,128]{1,0:T(8,128)S(1)}, u32[]{:S(2)}, u32[]{:S(2)}) collective-permute-start(f32[512,128]{1,0:T(8,128)S(1)} %get-tuple-element.36), channel_id=1, source_target_pairs={{0,15},{1,2},{2,1},{3,4},{4,3},{5,6},{6,5},{7,8},{8,7},{9,10},{10,... | collective-permute-start | bytes 786440 | tf_op jit(solution)/shard_map/ppermute | solution.py:284
  111.1 4.0 %collective-permute-start.21 = (f32[8,128]{1,0:T(8,128)S(1)}, f32[8,128]{1,0:T(8,128)S(1)}, u32[]{:S(2)}, u32[]{:S(2)}) collective-permute-start(f32[8,128]{1,0:T(8,128)S(1)} %max.16), channel_id=1, source_target_pairs={{0,4},{1,5},{2,6},{3,7},{4,0},{5,1},{6,2},{7,3},{8,12},{9,13},{10,... | collective-permute-start | bytes 12296 | tf_op jit(solution)/shard_map/ppermute | solution.py:18
  115.1 5.7 %collective-permute-start.22 = (f32[8,128]{1,0:T(8,128)S(1)}, f32[8,128]{1,0:T(8,128)S(1)}, u32[]{:S(2)}, u32[]{:S(2)}) collective-permute-start(f32[8,128]{1,0:T(8,128)S(1)} %max.17), channel_id=1, source_target_pairs={{0,8},{1,9},{2,10},{3,11},{4,12},{5,13},{6,14},{7,15},{8,0},{9,1},... | collective-permute-start | bytes 12296 | tf_op jit(solution)/shard_map/ppermute | solution.py:18
  (9 other events, 102.4 us)

commit v2 on v1

v2 whole, which is shorter than its diff:
```python
import functools
import math

import jax
import jax.numpy as jnp
from jax import lax
from jax.experimental import pallas as pl
from jax.experimental.pallas import tpu as pltpu
from jax.sharding import PartitionSpec as P


START = 40
LANE = 128
AXIS = "feat"


def swap(value, bit):
    count = lax.axis_size(AXIS)
    return lax.ppermute(value, AXIS, [(i, i ^ bit) for i in range(count)])


def stages(count):
    return [1 << s for s in range(count.bit_length() - 1)]


def halves(values):
    high = values.astype(jnp.bfloat16)
    low = (values - high.astype(jnp.float32)).astype(jnp.bfloat16)
    return high, low


def mul(left, right):
    return lax.dot_general(left, right, (((1,), (0,)), ((), ())), preferred_element_type=jnp.float32)


def shrink(values, level):
    return values - jnp.clip(values, -level, level)


def forward(high, low, point):
    width = point.shape[1]
    ph, plo = halves(point)
    both = mul(high, jnp.concatenate([ph, plo], axis=1))
    return both[:, :width] + both[:, width:] + mul(low, ph)


def backward(high, low, turned):
    width = turned.shape[0] // 2
    both = mul(turned, high)
    return both[:width] + both[width:] + mul(turned[:width], low)


def hand_over(parity, total, keep_ref, send_ref):
    half = keep_ref.shape[0]
    keep_ref[...] = total[pl.ds(pl.multiple_of(parity * half, 8), half), :]
    send_ref[...] = total[pl.ds(pl.multiple_of((1 - parity) * half, 8), half), :]


def take_over(parity, own_ref, other_ref, targets_ref, turned, whole):
    half = own_ref.shape[0]
    whole[pl.ds(pl.multiple_of(parity * half, 8), half), :] = own_ref[...]
    whole[pl.ds(pl.multiple_of((1 - parity) * half, 8), half), :] = other_ref[...]
    width = targets_ref.shape[1]
    misfit = whole[...] - targets_ref[...]
    across = misfit.T
    high, low = halves(across)
    turned[:width] = high
    turned[width:] = low
    return misfit


def mask_of(drop_ref, dest_ref, start, count, shard):
    mask = jnp.int32(0)
    for k in range(count):
        moves = (drop_ref[start + k] == 0) & (dest_ref[start + k] == shard)
        mask = mask + jnp.where(moves, jnp.int32(1 << k), jnp.int32(0))
    return mask


def first_kernel(
    push, shards, me_ref, drop_ref, dest_ref, design_ref, now_ref, prev_ref,
    keep_ref, send_ref, near_ref, far_a_ref, far_b_ref, total,
):
    step = pl.program_id(0)
    last = pl.num_programs(0) - 1
    me = me_ref[0]
    parity = me & 1
    block = design_ref[...]
    high, low = halves(block)
    now = now_ref[...]
    part = forward(high, low, now + push * (now - prev_ref[...]))
    rows = block.shape[0]
    edge = block.shape[1] // LANE
    blocks = drop_ref.shape[0]

    @pl.when(step == 0)
    def _():
        total[...] = part

    @pl.when(step > 0)
    def _():
        total[...] += part

    def flags(ref, right):
        if right:
            mask = mask_of(drop_ref, dest_ref, blocks - edge, edge, lax.rem(me + 1, shards))
        else:
            mask = mask_of(drop_ref, dest_ref, 0, edge, lax.rem(me + shards - 1, shards))
        size = ref.shape[0]
        ref[size - 8 :, :] = jnp.full((8, ref.shape[1]), mask.astype(jnp.float32), jnp.float32)

    def put_near(right):
        near_ref[:rows, :] = block
        flags(near_ref, right)

    def put_far(right):
        far_a_ref[: rows // 2, :] = block[: rows // 2]
        far_b_ref[...] = block[rows // 2 :]
        flags(far_a_ref, right)

    @pl.when((step == 0) & (parity == 1))
    def _():
        put_near(False)

    @pl.when((step == 0) & (parity == 0))
    def _():
        put_far(False)

    @pl.when((step == last) & (parity == 0))
    def _():
        put_near(True)

    @pl.when((step == last) & (parity == 1))
    def _():
        put_far(True)

    @pl.when(step == last)
    def _():
        hand_over(parity, total, keep_ref, send_ref)


def descend_kernel(
    push_in, push_out, scale, level_scale, parity_ref, design_ref, later_ref, early_ref, own_ref, other_ref, targets_ref,
    penalty_ref, coef_ref, keep_ref, send_ref, *rest,
):
    total, turned = rest[-2:]
    step = pl.program_id(0)
    last = pl.num_programs(0) - 1
    parity = parity_ref[0] & 1

    @pl.when(step == 0)
    def _():
        take_over(parity, own_ref, other_ref, targets_ref, turned, total)

    high, low = halves(design_ref[...])
    turn = backward(high, low, turned[...])
    later = later_ref[...]
    point = later + push_in * (later - early_ref[...])
    coef = shrink(point - turn.T * (1.0 / scale), penalty_ref[...] * level_scale)
    coef_ref[...] = coef
    if push_out is not None:
        part = forward(high, low, coef + push_out * (coef - later))
    else:
        part = forward(high, low, coef)
        mass_ref, near_ref, far_ref = rest[:3]
        mass = jnp.sum(jnp.abs(coef), axis=0, keepdims=True)

        @pl.when(step == 0)
        def _():
            mass_ref[...] = mass

        @pl.when(step > 0)
        def _():
            mass_ref[...] += mass

        @pl.when(((step == 0) & (parity == 1)) | ((step == last) & (parity == 0)))
        def _():
            near_ref[...] = coef

        @pl.when(((step == 0) & (parity == 0)) | ((step == last) & (parity == 1)))
        def _():
            far_ref[...] = coef

    @pl.when(step == 0)
    def _():
        total[...] = part

    @pl.when(step > 0)
    def _():
        total[...] += part

    @pl.when(step == last)
    def _():
        hand_over(parity, total, keep_ref, send_ref)


def peak_kernel(
    parity_ref, design_ref, own_ref, other_ref, targets_ref, mass_ref,
    peak_ref, square_ref, cross_ref, total, turned, best,
):
    step = pl.program_id(0)
    parity = parity_ref[0] & 1

    @pl.when(step == 0)
    def _():
        residual = -take_over(parity, own_ref, other_ref, targets_ref, turned, total)
        square_ref[...] = jnp.sum(residual * residual, axis=0, keepdims=True)
        cross_ref[...] = jnp.sum(residual * targets_ref[...], axis=0, keepdims=True)
        best[...] = jnp.zeros_like(best)

    high, low = halves(design_ref[...])
    turn = jnp.abs(backward(high, low, turned[...]))
    for k in range(turn.shape[1] // LANE):
        best[...] = jnp.maximum(best[...], turn[:, k * LANE : (k + 1) * LANE])

    @pl.when(step == pl.num_programs(0) - 1)
    def _():
        half = peak_ref.shape[0] // 2
        peak_ref[:half] = jnp.broadcast_to(jnp.max(best[...].T, axis=0, keepdims=True), (half, LANE))
        peak_ref[half:] = jnp.broadcast_to(mass_ref[...], (half, LANE))


def place_design_kernel(
    me_ref, drop_ref, dest_ref, near_ref, own_ref, far_a_ref, far_b_ref, out_ref, table_ref, blank, sems, more,
):
    blocks = drop_ref.shape[0]
    slots = table_ref.shape[0]
    edge = (slots - blocks) // 2
    rows = out_ref.shape[0]
    half = rows // 2
    me = me_ref[0]
    parity = me & 1
    near = jnp.max(near_ref[rows:, :LANE]).astype(jnp.int32)
    far = jnp.max(far_a_ref[half:, :LANE]).astype(jnp.int32)
    before = jnp.where(parity == 1, near, far)
    after = jnp.where(parity == 1, far, near)
    blank[...] = jnp.zeros_like(blank)

    def cols(ref, index):
        return ref.at[:, pl.ds(pl.multiple_of(index * LANE, LANE), LANE)]

    def cut(ref, first, count, index):
        return ref.at[first : first + count, pl.ds(pl.multiple_of(index * LANE, LANE), LANE)]

    def from_near(slot, index):
        pltpu.make_async_copy(cut(near_ref, 0, rows, index), cols(out_ref, slot), sems.at[slot]).start()
        return jnp.int32(0)

    def from_far(slot, index):
        pltpu.make_async_copy(cut(far_a_ref, 0, half, index), cut(out_ref, 0, half, slot), more.at[0, slot]).start()
        pltpu.make_async_copy(cut(far_b_ref, 0, half, index), cut(out_ref, half, half, slot), more.at[1, slot]).start()

    count = jnp.int32(0)
    for slot in range(slots):
        table_ref[slot] = jnp.int32(-1)
    for cand in range(slots):
        if cand < edge:
            here = (before >> cand) & 1
        elif cand < edge + blocks:
            k = cand - edge
            here = jnp.where((drop_ref[k] == 0) & (dest_ref[k] == me), jnp.int32(1), jnp.int32(0))
        else:
            here = (after >> (cand - edge - blocks)) & 1

        @pl.when(here == 1)
        def _(cand=cand, count=count):
            table_ref[count] = jnp.int32(cand)

        count = count + here

    def parts(slot):
        source = table_ref[slot]
        left = (source >= 0) & (source < edge)
        right = source >= edge + blocks
        inner = jnp.where(left, source, source - edge - blocks)
        near_side = (left & (parity == 1)) | (right & (parity == 0))
        far_side = (left & (parity == 0)) | (right & (parity == 1))
        return source, inner, near_side, far_side

    for slot in range(slots):
        source, inner, near_side, far_side = parts(slot)

        @pl.when(source < 0)
        def _(slot=slot):
            pltpu.make_async_copy(blank, cols(out_ref, slot), sems.at[slot]).start()

        @pl.when((source >= edge) & (source < edge + blocks))
        def _(slot=slot, source=source):
            pltpu.make_async_copy(cols(own_ref, source - edge), cols(out_ref, slot), sems.at[slot]).start()

        @pl.when(near_side)
        def _(slot=slot, inner=inner):
            from_near(slot, inner)

        @pl.when(far_side)
        def _(slot=slot, inner=inner):
            from_far(slot, inner)

    for slot in range(slots):
        far_side = parts(slot)[3]

        @pl.when(far_side)
        def _(slot=slot):
            for part, ref in enumerate((far_a_ref, far_b_ref)):
                pltpu.make_async_copy(cut(ref, 0, half, 0), cut(out_ref, part * half, half, slot), more.at[part, slot]).wait()

        @pl.when(jnp.logical_not(far_side))
        def _(slot=slot):
            pltpu.make_async_copy(blank, cols(out_ref, slot), sems.at[slot]).wait()


def place_coef_kernel(edge, me_ref, table_ref, near_ref, own_ref, far_ref, out_ref, blank, sems):
    slots = table_ref.shape[0]
    own = slots - 2 * edge
    parity = me_ref[0] & 1
    blank[...] = jnp.zeros_like(blank)

    def rows(ref, index):
        return ref.at[pl.ds(pl.multiple_of(index * LANE, LANE), LANE), :]

    def copy(slot, src):
        return pltpu.make_async_copy(src, rows(out_ref, slot), sems.at[slot])

    for slot in range(slots):
        source = table_ref[slot]
        left = (source >= 0) & (source < edge)
        right = source >= edge + own
        inner = jnp.where(left, source, source - edge - own)

        @pl.when(source < 0)
        def _(slot=slot):
            copy(slot, blank).start()

        @pl.when((source >= edge) & (source < edge + own))
        def _(slot=slot, source=source):
            copy(slot, rows(own_ref, source - edge)).start()

        @pl.when((left & (parity == 1)) | (right & (parity == 0)))
        def _(slot=slot, inner=inner):
            copy(slot, rows(near_ref, inner)).start()

        @pl.when((left & (parity == 0)) | (right & (parity == 1)))
        def _(slot=slot, inner=inner):
            copy(slot, rows(far_ref, inner)).start()

    for slot in range(slots):
        copy(slot, blank).wait()


VM = pltpu.MemorySpace.VMEM
SM = pltpu.MemorySpace.SMEM


def whole():
    return pl.BlockSpec(memory_space=VM)


def scalars():
    return pl.BlockSpec(memory_space=SM)


def f32(*shape):
    return jax.ShapeDtypeStruct(shape, jnp.float32)


def fixed(shape):
    return pl.BlockSpec(shape, lambda i: (0,) * len(shape))


def body(design, targets, coef_now, coef_prev, penalty, drop_mask, dest_shard):
    samples, feats = design.shape
    width = targets.shape[1]
    shards = lax.axis_size(AXIS)
    me = lax.axis_index(AXIS).astype(jnp.int32).reshape(1)
    lipschitz = (math.sqrt(samples) + math.sqrt(feats * shards)) ** 2
    first_push = (START - 1) / (START + 2)
    second_push = START / (START + 3)
    blocks = feats // LANE
    edge = blocks // 4
    slots = blocks + 2 * edge
    chunk = edge * LANE
    steps = feats // chunk
    half = samples // 2
    bits = stages(shards)

    def feat_spec():
        return pl.BlockSpec((samples, chunk), lambda i: (0, i))

    def coef_spec():
        return pl.BlockSpec((chunk, width), lambda i: (i, 0))

    params = pltpu.CompilerParams(vmem_limit_bytes=24 << 20, dimension_semantics=("arbitrary",))
    row_spec = fixed((1, width))
    half_spec = fixed((half, width))
    line = penalty.reshape(1, width)

    def in_hbm(value):
        return pltpu.with_memory_space_constraint(value, pltpu.MemorySpace.HBM)

    drop, dest = in_hbm(drop_mask), in_hbm(dest_shard)
    edge_shapes = [(samples + 8, chunk), (half + 8, chunk), (half, chunk)]
    keep, send, near, far_a, far_b = pl.pallas_call(
        functools.partial(first_kernel, first_push, shards),
        grid=(steps,),
        in_specs=[scalars(), scalars(), scalars(), feat_spec(), coef_spec(), coef_spec()],
        out_specs=[half_spec, half_spec] + [fixed(shape) for shape in edge_shapes],
        out_shape=[f32(half, width)] * 2 + [f32(*shape) for shape in edge_shapes],
        scratch_shapes=[pltpu.VMEM((samples, width), jnp.float32)],
        compiler_params=params,
        name="first",
    )(me, drop, dest, in_hbm(design), in_hbm(coef_now), in_hbm(coef_prev))

    def inward(value):
        return swap(value, 1)

    def outward(value):
        pairs = [(i, (i + 1) % shards if i % 2 else (i - 1) % shards) for i in range(shards)]
        return lax.ppermute(value, AXIS, pairs)

    def combine(keep, send):
        total = keep + swap(send, 1)
        for bit in bits[1:]:
            total = total + swap(total, bit)
        other = swap(total, 1)
        return total, other

    near_in = inward(near)
    far_a_in = outward(far_a)
    far_b_in = outward(far_b)

    turned = pltpu.VMEM((2 * width, samples), jnp.bfloat16)
    sum_scratch = pltpu.VMEM((samples, width), jnp.float32)

    def descend(push_in, push_out, later, early, own, other):
        out_specs = [coef_spec(), half_spec, half_spec]
        out_shape = [f32(feats, width), f32(half, width), f32(half, width)]
        if push_out is None:
            out_specs += [row_spec, fixed((chunk, width)), fixed((chunk, width))]
            out_shape += [f32(1, width), f32(chunk, width), f32(chunk, width)]
        return pl.pallas_call(
            functools.partial(descend_kernel, push_in, push_out, lipschitz, samples / lipschitz),
            grid=(steps,),
            in_specs=[scalars(), feat_spec(), coef_spec(), coef_spec(), half_spec, half_spec, fixed((samples, width)), row_spec],
            out_specs=out_specs,
            out_shape=out_shape,
            scratch_shapes=[sum_scratch, turned],
            compiler_params=params,
            name="descend",
        )(me, design, later, early, own, other, targets, line)

    own, other = combine(keep, send)
    coef_one, keep, send = descend(first_push, second_push, coef_now, coef_prev, own, other)
    own, other = combine(keep, send)
    coef_two, keep, send, mass, near, far = descend(second_push, None, coef_one, coef_now, own, other)
    near_coef = inward(near)
    far_coef = outward(far)
    own, other = combine(keep, send)

    design_out, table = pl.pallas_call(
        place_design_kernel,
        in_specs=[scalars(), scalars(), scalars(), whole(), whole(), whole(), whole()],
        out_specs=[pl.BlockSpec(memory_space=pl.ANY), scalars()],
        out_shape=[f32(samples, slots * LANE), jax.ShapeDtypeStruct((slots,), jnp.int32)],
        scratch_shapes=[
            pltpu.VMEM((samples, LANE), jnp.float32),
            pltpu.SemaphoreType.DMA((slots,)),
            pltpu.SemaphoreType.DMA((2, slots)),
        ],
        compiler_params=pltpu.CompilerParams(vmem_limit_bytes=24 << 20),
        name="place_design",
    )(me, drop, dest, near_in, design, far_a_in, far_b_in)

    tail, square, cross = pl.pallas_call(
        peak_kernel,
        grid=(steps,),
        in_specs=[scalars(), feat_spec(), half_spec, half_spec, fixed((samples, width)), row_spec],
        out_specs=[fixed((16, width)), row_spec, row_spec],
        out_shape=[f32(16, width), f32(1, width), f32(1, width)],
        scratch_shapes=[sum_scratch, turned, pltpu.VMEM((width, LANE), jnp.float32)],
        compiler_params=params,
        name="peak",
    )(me, design, own, other, targets, mass)
    is_peak = lax.broadcasted_iota(jnp.int32, (16, width), 0) < 8
    for bit in bits:
        got = swap(tail, bit)
        tail = jnp.where(is_peak, jnp.maximum(tail, got), tail + got)

    coef_out = pl.pallas_call(
        functools.partial(place_coef_kernel, edge),
        in_specs=[scalars(), scalars(), whole(), whole(), whole()],
        out_specs=pl.BlockSpec(memory_space=pl.ANY),
        out_shape=f32(slots * LANE, width),
        scratch_shapes=[pltpu.VMEM((LANE, width), jnp.float32), pltpu.SemaphoreType.DMA((slots,))],
        compiler_params=pltpu.CompilerParams(vmem_limit_bytes=24 << 20),
        name="place_coef",
    )(me, table, near_coef, coef_two, far_coef)

    peak, mass = tail[0], tail[8]
    dual_scale = jnp.maximum(penalty, peak / samples)
    ratio = penalty / dual_scale
    dual_value = (2.0 * ratio * cross[0] - ratio * ratio * square[0]) / (2.0 * samples)
    duality_gap = square[0] / (2.0 * samples) + penalty * mass - dual_value
    return (coef_out, design_out, duality_gap, dual_value, mass)


def solution(mesh):
    placed = (
        P("groups", "feat"),
        P("groups", None),
        P(("groups", "feat"), None),
        P(("groups", "feat"), None),
        P("groups"),
        P(("groups", "feat")),
        P(("groups", "feat")),
    )
    return jax.shard_map(
        body,
        mesh=mesh,
        in_specs=placed,
        out_specs=(
            P(("groups", "feat"), None),
            P("groups", "feat"),
            P("groups"),
            P("groups"),
            P("groups"),
        ),
        check_vma=False,
    )
```

time: 122 us -> 119 us (0.975)
  waiting for transfers between devices: 59.4 us -> 72.1 us
  local copies, waits for them, and re-layouts: 8.42 us -> 0.03 us
  starting transfers between devices: 26.6 us -> 22.5 us
  other arithmetic: 5.07 us -> 1.05 us
    ppermute x21, waiting for transfers between devices: 59.4 us -> 70.4 us  [swap(): return lax.ppermute(value, AXIS, [(i, i ^ bit) for i in range(count)])]
    unnamed x20 -> x10, local copies, waits for them, and re-layouts: 7.49 us -> 0.03 us
    ppermute x21, starting transfers between devices: 18.6 us -> 16 us  [swap(): return lax.ppermute(value, AXIS, [(i, i ^ bit) for i in range(count)])]
    ppermute x2 -> x3, waiting for transfers between devices: 0.01 us -> 1.73 us  [outward(): return lax.ppermute(value, AXIS, pairs)]
    add x9, other arithmetic: 1.77 us -> 0.17 us  [combine(): total = total + swap(total, bit)]
    ppermute x2 -> x3, starting transfers between devices: 8.03 us -> 6.45 us  [outward(): return lax.ppermute(value, AXIS, pairs)]
    and x2 -> x0, other arithmetic: 1.49 us -> none  [the longest x1 0.81 us: local(): to_left = survive[:edge] & (dest_shard[:edge] == (me + shards - 1) % shards)]
  transfers between devices with their start and end apart: 23 -> 24, of which waited for: 17 -> 18; matrix products, arithmetic and copies ran while one was open for 1% -> 0% of each run, Pallas kernels for 8% -> 7%
where the time goes in v2:
time: 119 us
  waiting for transfers between devices  72.1 us (61%)
  starting transfers between devices  22.5 us (19%)
  Pallas kernels  22.3 us (19%)
    ppermute x21, waiting for transfers between devices, swap(): return lax.ppermute(value, AXIS, [(i, i ^ bit) for i in range(count)])  70.4 us
    ppermute x21, starting transfers between devices, swap(): return lax.ppermute(value, AXIS, [(i, i ^ bit) for i in range(count)])  16 us
    pallas_call x2, Pallas kernels, descend(): pl.pallas_call(functools.partial(descend_kernel, push_in, push_out, lipsc...  8.55 us
    ppermute x3, starting transfers between devices, outward(): return lax.ppermute(value, AXIS, pairs)  6.45 us
    pallas_call x1, Pallas kernels, body(): pl.pallas_call(functools.partial(first_kernel, first_push, shards), grid=...  5.01 us
    pallas_call x1, Pallas kernels, body(): pl.pallas_call(place_design_kernel, in_specs=[scalars(), scalars(), scala...  4.72 us
  transfers between devices with their start and end apart: 24, of which 18 were waited for; matrix products, arithmetic and copies ran while one was open for 0% of the time, Pallas kernels for 7%

profile of v2, /device:TPU:0, one launch (start us, length us, event | category | flops | bytes accessed | tf_op | source)
XLA Modules:
  0.0 118.9 jit_solution(1142107997588847576)
XLA Ops:
  0.7 5.0 %first.1 = (f32[256,128]{1,0:T(8,128)S(1)}, f32[256,128]{1,0:T(8,128)S(1)}, f32[520,512]{1,0:T(8,128)S(1)}, f32[264,512]{1,0:T(8,128)S(1)}, f32[256,512]{1,0:T(8,128)S(1)}) custom-call(s32[1]{0:T(128)} %bitcast.me_ref.parity_ref, s32[16]{0:T(128)} %drop_ref.3, s32[16]{0:T(128)} %dest_ref.3, f32[512,2048]{1,0:T(8,128)} %design_ref.7, f32[2048,128]{1,0:T(8,128)} %early_ref.3, ...), custom_call_target="tpu_custom_call" | custom-call | tf_op jit(solution)/shard_map/first/pallas_call | solution.py:402
  7.3 2.9 %collective-permute-start.4 = (f32[256,128]{1,0:T(8,128)S(1)}, f32[256,128]{1,0:T(8,128)S(1)}, u32[]{:S(2)}, u32[]{:S(2)}) collective-permute-start(f32[256,128]{1,0:T(8,128)S(1)} %add.51), channel_id=1, source_target_pairs={{0,2},{1,3},{2,0},{3,1},{4,6},{5,7},{6,4},{7,5},{8,10},{9,11},{10,... | collective-permute-start | bytes 393224 | tf_op jit(solution)/shard_map/ppermute | solution.py:19
  10.2 3.8 %collective-permute-done.4 = f32[256,128]{1,0:T(8,128)S(1)} collective-permute-done((f32[256,128]{1,0:T(8,128)S(1)}, f32[256,128]{1,0:T(8,128)S(1)}, u32[]{:S(2)}, u32[]{:S(2)}) %collective-permute-start.4) | collective-permute-done | bytes 131104 | tf_op jit(solution)/shard_map/ppermute | solution.py:19
  14.0 1.9 %collective-permute-start.5 = (f32[256,128]{1,0:T(8,128)S(1)}, f32[256,128]{1,0:T(8,128)S(1)}, u32[]{:S(2)}, u32[]{:S(2)}) collective-permute-start(f32[256,128]{1,0:T(8,128)S(1)} %add.52), channel_id=1, source_target_pairs={{0,4},{1,5},{2,6},{3,7},{4,0},{5,1},{6,2},{7,3},{8,12},{9,13},{10,... | collective-permute-start | bytes 393224 | tf_op jit(solution)/shard_map/ppermute | solution.py:19
  15.9 3.2 %collective-permute-done.5 = f32[256,128]{1,0:T(8,128)S(1)} collective-permute-done((f32[256,128]{1,0:T(8,128)S(1)}, f32[256,128]{1,0:T(8,128)S(1)}, u32[]{:S(2)}, u32[]{:S(2)}) %collective-permute-start.5) | collective-permute-done | bytes 131104 | tf_op jit(solution)/shard_map/ppermute | solution.py:19
  19.1 2.9 %collective-permute-start.6 = (f32[256,128]{1,0:T(8,128)S(1)}, f32[256,128]{1,0:T(8,128)S(1)}, u32[]{:S(2)}, u32[]{:S(2)}) collective-permute-start(f32[256,128]{1,0:T(8,128)S(1)} %add.53), channel_id=1, source_target_pairs={{0,8},{1,9},{2,10},{3,11},{4,12},{5,13},{6,14},{7,15},{8,0},{9,1},... | collective-permute-start | bytes 393224 | tf_op jit(solution)/shard_map/ppermute | solution.py:19
  22.0 5.0 %collective-permute-done.6 = f32[256,128]{1,0:T(8,128)S(1)} collective-permute-done((f32[256,128]{1,0:T(8,128)S(1)}, f32[256,128]{1,0:T(8,128)S(1)}, u32[]{:S(2)}, u32[]{:S(2)}) %collective-permute-start.6) | collective-permute-done | bytes 131104 | tf_op jit(solution)/shard_map/ppermute | solution.py:19
  28.4 4.2 %descend.2 = (f32[2048,128]{1,0:T(8,128)S(1)}, f32[256,128]{1,0:T(8,128)S(1)}, f32[256,128]{1,0:T(8,128)S(1)}) custom-call(s32[1]{0:T(128)} %bitcast.me_ref.parity_ref, f32[512,2048]{1,0:T(8,128)S(1)} %copy-done, f32[2048,128]{1,0:T(8,128)S(1)} %copy-done.1, f32[2048,128]{1,0:T(8,128)S(1)} %copy-done.2, f32[256,128]{1,0:T(8,128)S(1)} %add.54.own_ref, ...), custom_call_target="tpu_custom_call" | custom-call | tf_op jit(solution)/shard_map/descend/pallas_call | solution.py:440
  35.4 4.4 %collective-permute-done.9 = f32[256,128]{1,0:T(8,128)S(1)} collective-permute-done((f32[256,128]{1,0:T(8,128)S(1)}, f32[256,128]{1,0:T(8,128)S(1)}, u32[]{:S(2)}, u32[]{:S(2)}) %collective-permute-start.9) | collective-permute-done | bytes 131104 | tf_op jit(solution)/shard_map/ppermute | solution.py:19
  40.1 4.6 %collective-permute-done.10 = f32[256,128]{1,0:T(8,128)S(1)} collective-permute-done((f32[256,128]{1,0:T(8,128)S(1)}, f32[256,128]{1,0:T(8,128)S(1)}, u32[]{:S(2)}, u32[]{:S(2)}) %collective-permute-start.10) | collective-permute-done | bytes 131104 | tf_op jit(solution)/shard_map/ppermute | solution.py:19
  44.8 1.8 %collective-permute-start.11 = (f32[256,128]{1,0:T(8,128)S(1)}, f32[256,128]{1,0:T(8,128)S(1)}, u32[]{:S(2)}, u32[]{:S(2)}) collective-permute-start(f32[256,128]{1,0:T(8,128)S(1)} %add.57), channel_id=1, source_target_pairs={{0,8},{1,9},{2,10},{3,11},{4,12},{5,13},{6,14},{7,15},{8,0},{9,1},... | collective-permute-start | bytes 393224 | tf_op jit(solution)/shard_map/ppermute | solution.py:19
  46.6 5.6 %collective-permute-done.11 = f32[256,128]{1,0:T(8,128)S(1)} collective-permute-done((f32[256,128]{1,0:T(8,128)S(1)}, f32[256,128]{1,0:T(8,128)S(1)}, u32[]{:S(2)}, u32[]{:S(2)}) %collective-permute-start.11) | collective-permute-done | bytes 131104 | tf_op jit(solution)/shard_map/ppermute | solution.py:19
  53.6 4.3 %descend.3 = (f32[2048,128]{1,0:T(8,128)S(1)}, f32[256,128]{1,0:T(8,128)S(1)}, f32[256,128]{1,0:T(8,128)S(1)}, f32[1,128]{1,0:T(1,128)S(1)}, f32[512,128]{1,0:T(8,128)S(1)}, /*index=5*/f32[512,128]{1,0:T(8,128)S(1)}) custom-call(s32[1]{0:T(128)} %bitcast.me_ref.parity_ref, f32[512,2048]{1,0:T(8,128)S(1)} %copy-done, ...), custom_call_target="tpu_custom_call" | custom-call | tf_op jit(solution)/shard_map/descend/pallas_call | solution.py:440
  60.6 4.4 %collective-permute-done.16 = f32[256,128]{1,0:T(8,128)S(1)} collective-permute-done((f32[256,128]{1,0:T(8,128)S(1)}, f32[256,128]{1,0:T(8,128)S(1)}, u32[]{:S(2)}, u32[]{:S(2)}) %collective-permute-start.16) | collective-permute-done | bytes 131104 | tf_op jit(solution)/shard_map/ppermute | solution.py:19
  65.4 4.7 %collective-permute-done.17 = f32[256,128]{1,0:T(8,128)S(1)} collective-permute-done((f32[256,128]{1,0:T(8,128)S(1)}, f32[256,128]{1,0:T(8,128)S(1)}, u32[]{:S(2)}, u32[]{:S(2)}) %collective-permute-start.17) | collective-permute-done | bytes 131104 | tf_op jit(solution)/shard_map/ppermute | solution.py:19
  70.0 1.8 %collective-permute-start.18 = (f32[256,128]{1,0:T(8,128)S(1)}, f32[256,128]{1,0:T(8,128)S(1)}, u32[]{:S(2)}, u32[]{:S(2)}) collective-permute-start(f32[256,128]{1,0:T(8,128)S(1)} %add.61), channel_id=1, source_target_pairs={{0,8},{1,9},{2,10},{3,11},{4,12},{5,13},{6,14},{7,15},{8,0},{9,1},... | collective-permute-start | bytes 393224 | tf_op jit(solution)/shard_map/ppermute | solution.py:19
  71.8 5.6 %collective-permute-done.18 = f32[256,128]{1,0:T(8,128)S(1)} collective-permute-done((f32[256,128]{1,0:T(8,128)S(1)}, f32[256,128]{1,0:T(8,128)S(1)}, u32[]{:S(2)}, u32[]{:S(2)}) %collective-permute-start.18) | collective-permute-done | bytes 131104 | tf_op jit(solution)/shard_map/ppermute | solution.py:19
  77.5 4.2 %collective-permute-start.1 = (f32[264,512]{1,0:T(8,128)S(1)}, f32[264,512]{1,0:T(8,128)S(1)}, u32[]{:S(2)}, u32[]{:S(2)}) collective-permute-start(f32[264,512]{1,0:T(8,128)S(1)} %get-tuple-element.25), channel_id=1, source_target_pairs={{0,15},{1,2},{2,1},{3,4},{4,3},{5,6},{6,5},{7,8},{8,7},{9,10},{10,... | collective-permute-start | bytes 1622024 | tf_op jit(solution)/shard_map/ppermute | solution.py:418
  82.0 2.2 %peak.1 = (f32[16,128]{1,0:T(8,128)S(1)}, f32[1,128]{1,0:T(1,128)S(1)}, f32[1,128]{1,0:T(1,128)S(1)}) custom-call(s32[1]{0:T(128)} %bitcast.me_ref.parity_ref, f32[512,2048]{1,0:T(8,128)S(1)} %copy-done, f32[256,128]{1,0:T(8,128)S(1)} %add.62.own_ref, f32[256,128]{1,0:T(8,128)S(1)} %collective-permute-done.19.other_ref, f32[512,128]{1,0:T(8,128)S(1)} %copy-done.3, ...), custom_call_target="tpu_custom_call" | custom-call | tf_op jit(solution)/shard_map/peak/pallas_call | solution.py:473
  85.5 18.6 %collective-permute-done.21 = f32[16,128]{1,0:T(8,128)S(1)} collective-permute-done((f32[16,128]{1,0:T(8,128)S(1)}, f32[16,128]{1,0:T(8,128)S(1)}, u32[]{:S(2)}, u32[]{:S(2)}) %collective-permute-start.21) | collective-permute-done | bytes 8224 | tf_op jit(solution)/shard_map/ppermute | solution.py:19
  104.5 3.3 %collective-permute-done.22 = f32[16,128]{1,0:T(8,128)S(1)} collective-permute-done((f32[16,128]{1,0:T(8,128)S(1)}, f32[16,128]{1,0:T(8,128)S(1)}, u32[]{:S(2)}, u32[]{:S(2)}) %collective-permute-start.22) | collective-permute-done | bytes 8224 | tf_op jit(solution)/shard_map/ppermute | solution.py:19
  107.9 1.9 %collective-permute-start.14 = (f32[512,128]{1,0:T(8,128)S(1)}, f32[512,128]{1,0:T(8,128)S(1)}, u32[]{:S(2)}, u32[]{:S(2)}) collective-permute-start(f32[512,128]{1,0:T(8,128)S(1)} %get-tuple-element.35), channel_id=1, source_target_pairs={{0,15},{1,2},{2,1},{3,4},{4,3},{5,6},{6,5},{7,8},{8,7},{9,10},{10,... | collective-permute-start | bytes 786440 | tf_op jit(solution)/shard_map/ppermute | solution.py:418
  109.9 4.7 %place_design.1 = (f32[512,3072]{1,0:T(8,128)}, s32[24]{0:T(128)S(1)}) custom-call(s32[1]{0:T(128)} %bitcast.me_ref.parity_ref, s32[16]{0:T(128)} %drop_ref.3, s32[16]{0:T(128)} %dest_ref.3, f32[520,512]{1,0:T(8,128)S(1)} %collective-permute-done.near_ref, f32[512,2048]{1,0:T(8,128)S(1)} %copy-done, f32[264,512]{1,0:T(8,128)S(1)} %collective-permute-done.1.far_a_ref, ...), custom_call_target="tpu_custom_call" | custom-call | tf_op jit(solution)/shard_map/place_design/pallas_call | solution.py:459
  116.4 1.9 %place_coef.1 = f32[3072,128]{1,0:T(8,128)} custom-call(s32[1]{0:T(128)} %bitcast.me_ref.parity_ref, s32[24]{0:T(128)S(1)} %get-tuple-element.27.table_ref, f32[512,128]{1,0:T(8,128)S(1)} %collective-permute-done.13.near_ref, f32[2048,128]{1,0:T(8,128)S(1)} %get-tuple-element.34.own_ref, f32[512,128]{1,0:T(8,128)S(1)} %collective-permute-done.14.far_ref), custom_call_target="tpu_custom_call" | custom-call | tf_op jit(solution)/shard_map/place_coef/pallas_call | solution.py:488
  (58 shorter events, 15.2 us)
Async XLA Ops:
  5.7 1.5 %collective-permute-start.3 = (f32[256,128]{1,0:T(8,128)S(1)}, f32[256,128]{1,0:T(8,128)S(1)}, u32[]{:S(2)}, u32[]{:S(2)}) collective-permute-start(f32[256,128]{1,0:T(8,128)S(1)} %get-tuple-element.29), channel_id=1, source_target_pairs={{0,1},{1,0},{2,3},{3,2},{4,5},{5,4},{6,7},{7,6},{8,9},{9,8},{10,11... | collective-permute-start | bytes 393224 | tf_op jit(solution)/shard_map/ppermute | solution.py:19
  7.3 6.7 %collective-permute-start.4 = (f32[256,128]{1,0:T(8,128)S(1)}, f32[256,128]{1,0:T(8,128)S(1)}, u32[]{:S(2)}, u32[]{:S(2)}) collective-permute-start(f32[256,128]{1,0:T(8,128)S(1)} %add.51), channel_id=1, source_target_pairs={{0,2},{1,3},{2,0},{3,1},{4,6},{5,7},{6,4},{7,5},{8,10},{9,11},{10,... | collective-permute-start | bytes 393224 | tf_op jit(solution)/shard_map/ppermute | solution.py:19
  14.0 5.0 %collective-permute-start.5 = (f32[256,128]{1,0:T(8,128)S(1)}, f32[256,128]{1,0:T(8,128)S(1)}, u32[]{:S(2)}, u32[]{:S(2)}) collective-permute-start(f32[256,128]{1,0:T(8,128)S(1)} %add.52), channel_id=1, source_target_pairs={{0,4},{1,5},{2,6},{3,7},{4,0},{5,1},{6,2},{7,3},{8,12},{9,13},{10,... | collective-permute-start | bytes 393224 | tf_op jit(solution)/shard_map/ppermute | solution.py:19
  19.1 7.9 %collective-permute-start.6 = (f32[256,128]{1,0:T(8,128)S(1)}, f32[256,128]{1,0:T(8,128)S(1)}, u32[]{:S(2)}, u32[]{:S(2)}) collective-permute-start(f32[256,128]{1,0:T(8,128)S(1)} %add.53), channel_id=1, source_target_pairs={{0,8},{1,9},{2,10},{3,11},{4,12},{5,13},{6,14},{7,15},{8,0},{9,1},... | collective-permute-start | bytes 393224 | tf_op jit(solution)/shard_map/ppermute | solution.py:19
  27.0 1.4 %collective-permute-start.7 = (f32[256,128]{1,0:T(8,128)S(1)}, f32[256,128]{1,0:T(8,128)S(1)}, u32[]{:S(2)}, u32[]{:S(2)}) collective-permute-start(f32[256,128]{1,0:T(8,128)S(1)} %add.54.own_ref), channel_id=1, source_target_pairs={{0,1},{1,0},{2,3},{3,2},{4,5},{5,4},{6,7},{7,6},{8,9},{9,8},{10,11... | collective-permute-start | bytes 393224 | tf_op jit(solution)/shard_map/ppermute | solution.py:19
  32.7 1.4 %collective-permute-start.8 = (f32[256,128]{1,0:T(8,128)S(1)}, f32[256,128]{1,0:T(8,128)S(1)}, u32[]{:S(2)}, u32[]{:S(2)}) collective-permute-start(f32[256,128]{1,0:T(8,128)S(1)} %get-tuple-element.32), channel_id=1, source_target_pairs={{0,1},{1,0},{2,3},{3,2},{4,5},{5,4},{6,7},{7,6},{8,9},{9,8},{10,11... | collective-permute-start | bytes 393224 | tf_op jit(solution)/shard_map/ppermute | solution.py:19
  34.1 5.6 %collective-permute-start.9 = (f32[256,128]{1,0:T(8,128)S(1)}, f32[256,128]{1,0:T(8,128)S(1)}, u32[]{:S(2)}, u32[]{:S(2)}) collective-permute-start(f32[256,128]{1,0:T(8,128)S(1)} %add.55), channel_id=1, source_target_pairs={{0,2},{1,3},{2,0},{3,1},{4,6},{5,7},{6,4},{7,5},{8,10},{9,11},{10,... | collective-permute-start | bytes 393224 | tf_op jit(solution)/shard_map/ppermute | solution.py:19
  39.8 5.0 %collective-permute-start.10 = (f32[256,128]{1,0:T(8,128)S(1)}, f32[256,128]{1,0:T(8,128)S(1)}, u32[]{:S(2)}, u32[]{:S(2)}) collective-permute-start(f32[256,128]{1,0:T(8,128)S(1)} %add.56), channel_id=1, source_target_pairs={{0,4},{1,5},{2,6},{3,7},{4,0},{5,1},{6,2},{7,3},{8,12},{9,13},{10,... | collective-permute-start | bytes 393224 | tf_op jit(solution)/shard_map/ppermute | solution.py:19
  44.8 7.3 %collective-permute-start.11 = (f32[256,128]{1,0:T(8,128)S(1)}, f32[256,128]{1,0:T(8,128)S(1)}, u32[]{:S(2)}, u32[]{:S(2)}) collective-permute-start(f32[256,128]{1,0:T(8,128)S(1)} %add.57), channel_id=1, source_target_pairs={{0,8},{1,9},{2,10},{3,11},{4,12},{5,13},{6,14},{7,15},{8,0},{9,1},... | collective-permute-start | bytes 393224 | tf_op jit(solution)/shard_map/ppermute | solution.py:19
  52.2 1.4 %collective-permute-start.12 = (f32[256,128]{1,0:T(8,128)S(1)}, f32[256,128]{1,0:T(8,128)S(1)}, u32[]{:S(2)}, u32[]{:S(2)}) collective-permute-start(f32[256,128]{1,0:T(8,128)S(1)} %add.58.own_ref), channel_id=1, source_target_pairs={{0,1},{1,0},{2,3},{3,2},{4,5},{5,4},{6,7},{7,6},{8,9},{9,8},{10,11... | collective-permute-start | bytes 393224 | tf_op jit(solution)/shard_map/ppermute | solution.py:19
  57.9 1.4 %collective-permute-start.15 = (f32[256,128]{1,0:T(8,128)S(1)}, f32[256,128]{1,0:T(8,128)S(1)}, u32[]{:S(2)}, u32[]{:S(2)}) collective-permute-start(f32[256,128]{1,0:T(8,128)S(1)} %get-tuple-element.38), channel_id=1, source_target_pairs={{0,1},{1,0},{2,3},{3,2},{4,5},{5,4},{6,7},{7,6},{8,9},{9,8},{10,11... | collective-permute-start | bytes 393224 | tf_op jit(solution)/shard_map/ppermute | solution.py:19
  59.3 5.6 %collective-permute-start.16 = (f32[256,128]{1,0:T(8,128)S(1)}, f32[256,128]{1,0:T(8,128)S(1)}, u32[]{:S(2)}, u32[]{:S(2)}) collective-permute-start(f32[256,128]{1,0:T(8,128)S(1)} %add.59), channel_id=1, source_target_pairs={{0,2},{1,3},{2,0},{3,1},{4,6},{5,7},{6,4},{7,5},{8,10},{9,11},{10,... | collective-permute-start | bytes 393224 | tf_op jit(solution)/shard_map/ppermute | solution.py:19
  65.0 5.0 %collective-permute-start.17 = (f32[256,128]{1,0:T(8,128)S(1)}, f32[256,128]{1,0:T(8,128)S(1)}, u32[]{:S(2)}, u32[]{:S(2)}) collective-permute-start(f32[256,128]{1,0:T(8,128)S(1)} %add.60), channel_id=1, source_target_pairs={{0,4},{1,5},{2,6},{3,7},{4,0},{5,1},{6,2},{7,3},{8,12},{9,13},{10,... | collective-permute-start | bytes 393224 | tf_op jit(solution)/shard_map/ppermute | solution.py:19
  70.0 7.3 %collective-permute-start.18 = (f32[256,128]{1,0:T(8,128)S(1)}, f32[256,128]{1,0:T(8,128)S(1)}, u32[]{:S(2)}, u32[]{:S(2)}) collective-permute-start(f32[256,128]{1,0:T(8,128)S(1)} %add.61), channel_id=1, source_target_pairs={{0,8},{1,9},{2,10},{3,11},{4,12},{5,13},{6,14},{7,15},{8,0},{9,1},... | collective-permute-start | bytes 393224 | tf_op jit(solution)/shard_map/ppermute | solution.py:19
  71.8 38.1 %collective-permute-start = (f32[520,512]{1,0:T(8,128)S(1)}, f32[520,512]{1,0:T(8,128)S(1)}, u32[]{:S(2)}, u32[]{:S(2)}) collective-permute-start(f32[520,512]{1,0:T(8,128)S(1)} %get-tuple-element.24), channel_id=1, source_target_pairs={{0,1},{1,0},{2,3},{3,2},{4,5},{5,4},{6,7},{7,6},{8,9},{9,8},{10,11... | collective-permute-start | bytes 3194888 | tf_op jit(solution)/shard_map/ppermute | solution.py:19
  77.4 4.6 %collective-permute-start.19 = (f32[256,128]{1,0:T(8,128)S(1)}, f32[256,128]{1,0:T(8,128)S(1)}, u32[]{:S(2)}, u32[]{:S(2)}) collective-permute-start(f32[256,128]{1,0:T(8,128)S(1)} %add.62.own_ref), channel_id=1, source_target_pairs={{0,1},{1,0},{2,3},{3,2},{4,5},{5,4},{6,7},{7,6},{8,9},{9,8},{10,11... | collective-permute-start | bytes 393224 | tf_op jit(solution)/shard_map/ppermute | solution.py:19
  77.5 32.4 %collective-permute-start.1 = (f32[264,512]{1,0:T(8,128)S(1)}, f32[264,512]{1,0:T(8,128)S(1)}, u32[]{:S(2)}, u32[]{:S(2)}) collective-permute-start(f32[264,512]{1,0:T(8,128)S(1)} %get-tuple-element.25), channel_id=1, source_target_pairs={{0,15},{1,2},{2,1},{3,4},{4,3},{5,6},{6,5},{7,8},{8,7},{9,10},{10,... | collective-permute-start | bytes 1622024 | tf_op jit(solution)/shard_map/ppermute | solution.py:418
  81.6 28.2 %collective-permute-start.2 = (f32[256,512]{1,0:T(8,128)S(1)}, f32[256,512]{1,0:T(8,128)S(1)}, u32[]{:S(2)}, u32[]{:S(2)}) collective-permute-start(f32[256,512]{1,0:T(8,128)S(1)} %get-tuple-element.26), channel_id=1, source_target_pairs={{0,15},{1,2},{2,1},{3,4},{4,3},{5,6},{6,5},{7,8},{8,7},{9,10},{10,... | collective-permute-start | bytes 1572872 | tf_op jit(solution)/shard_map/ppermute | solution.py:418
  84.2 1.2 %collective-permute-start.20 = (f32[16,128]{1,0:T(8,128)S(1)}, f32[16,128]{1,0:T(8,128)S(1)}, u32[]{:S(2)}, u32[]{:S(2)}) collective-permute-start(f32[16,128]{1,0:T(8,128)S(1)} %get-tuple-element.41), channel_id=1, source_target_pairs={{0,1},{1,0},{2,3},{3,2},{4,5},{5,4},{6,7},{7,6},{8,9},{9,8},{10,11... | collective-permute-start | bytes 24584 | tf_op jit(solution)/shard_map/ppermute | solution.py:19
  85.5 18.7 %collective-permute-start.21 = (f32[16,128]{1,0:T(8,128)S(1)}, f32[16,128]{1,0:T(8,128)S(1)}, u32[]{:S(2)}, u32[]{:S(2)}) collective-permute-start(f32[16,128]{1,0:T(8,128)S(1)} %add_select_fusion.3), channel_id=1, source_target_pairs={{0,2},{1,3},{2,0},{3,1},{4,6},{5,7},{6,4},{7,5},{8,10},{9,11},{10,... | collective-permute-start | bytes 24584 | tf_op jit(solution)/shard_map/ppermute | solution.py:19
  104.2 3.7 %collective-permute-start.22 = (f32[16,128]{1,0:T(8,128)S(1)}, f32[16,128]{1,0:T(8,128)S(1)}, u32[]{:S(2)}, u32[]{:S(2)}) collective-permute-start(f32[16,128]{1,0:T(8,128)S(1)} %add_select_fusion.2), channel_id=1, source_target_pairs={{0,4},{1,5},{2,6},{3,7},{4,0},{5,1},{6,2},{7,3},{8,12},{9,13},{10,... | collective-permute-start | bytes 24584 | tf_op jit(solution)/shard_map/ppermute | solution.py:19
  104.5 10.1 %collective-permute-start.13 = (f32[512,128]{1,0:T(8,128)S(1)}, f32[512,128]{1,0:T(8,128)S(1)}, u32[]{:S(2)}, u32[]{:S(2)}) collective-permute-start(f32[512,128]{1,0:T(8,128)S(1)} %get-tuple-element.33), channel_id=1, source_target_pairs={{0,1},{1,0},{2,3},{3,2},{4,5},{5,4},{6,7},{7,6},{8,9},{9,8},{10,11... | collective-permute-start | bytes 786440 | tf_op jit(solution)/shard_map/ppermute | solution.py:19
  107.9 8.5 %collective-permute-start.14 = (f32[512,128]{1,0:T(8,128)S(1)}, f32[512,128]{1,0:T(8,128)S(1)}, u32[]{:S(2)}, u32[]{:S(2)}) collective-permute-start(f32[512,128]{1,0:T(8,128)S(1)} %get-tuple-element.35), channel_id=1, source_target_pairs={{0,15},{1,2},{2,1},{3,4},{4,3},{5,6},{6,5},{7,8},{8,7},{9,10},{10,... | collective-permute-start | bytes 786440 | tf_op jit(solution)/shard_map/ppermute | solution.py:418
  109.9 8.4 %collective-permute-start.23 = (f32[16,128]{1,0:T(8,128)S(1)}, f32[16,128]{1,0:T(8,128)S(1)}, u32[]{:S(2)}, u32[]{:S(2)}) collective-permute-start(f32[16,128]{1,0:T(8,128)S(1)} %add_select_fusion.1), channel_id=1, source_target_pairs={{0,8},{1,9},{2,10},{3,11},{4,12},{5,13},{6,14},{7,15},{8,0},{9,1},... | collective-permute-start | bytes 24584 | tf_op jit(solution)/shard_map/ppermute | solution.py:19
  (5 other events, 123.8 us)
